TPU v7x, 32 devices: a whole 2x2x4 slice. The times are simulated.
32 devices in a mesh: groups: 2 (over y), bricks: 4 (over z), chan: 2 (over x), rep: 2 (over core).
Axes of the slice: x: 2, y: 2, z: 4, core: 2. Of those that a mesh axis runs over, the one named last changes fastest.
Arguments:
- features: bfloat16 [16, 64, 8, 24, 128], P(('groups', 'bricks', 'rep')), parts along dimension 0, may hold values from -6 to 6
- w_first: bfloat16 [27, 64, 64], P(None, None, 'chan'), may hold values from -0.15625 to 0.15625
- w_second: bfloat16 [27, 64, 64], P(None, None, 'chan'), may hold values from -0.15625 to 0.15625
- w_down: bfloat16 [8, 64, 64], P(None, 'chan'), may hold values from -0.25 to 0.25
- w_head: float32 [64], replicated, may hold values from -0.75 to 0.75
- footprint: int32 [2, 16], P(None, 'groups'), parts along dimension 1, may hold values from 0 to 3, as said below
- labels: int32 [16, 4, 768], P(('groups', 'bricks', 'rep')), parts along dimension 0, may hold values 0 or 1
Outputs:
- grad_second: float32 [54, 64, 64], P('groups', None, 'chan'), parts along dimension 0
- grad_down: float32 [16, 64, 64], P('groups', 'chan'), parts along dimension 0
- grad_head: float32 [128], P('groups'), parts along dimension 0
- loss: float32 [2], P('groups'), parts along dimension 0
There are 2 independent parts, one for each index of `groups`. A program takes and returns all parts, laid end to end along the dimension named above; an argument that names none is the same for every part. Nothing has to cross between parts.
Inputs may be any that keep to these rules, and one draw needn't show every extreme that they name: `footprint`: row 0 gives each column's first live brick row, 0 or 1; row 1 its number of live bricks. Columns 2k and 2k + 1 hold 2 to 4 live bricks together, and some column holds 3.
All inputs are finite; a program needn't handle non-finite values. No bound on the sum of `labels` on one device may be relied on, other than what follows from the above.
Results may differ from a plain program's by a relative error of at most 0.0035.
Values may be sent and summed in bfloat16 or wider, within the bound.
No kernel may reach another device: no remote copies, remote signals or barrier semaphores. Data moves between devices by JAX's collectives and lax.ppermute only.
A program may use at most 128 MiB of HBM per device.

v0:
```python
import functools

import jax
import jax.numpy as jnp
from jax import lax
from jax.experimental import pallas as pl
from jax.experimental.pallas import tpu as pltpu
from jax.sharding import PartitionSpec as P

BRICK = 8
COARSE = 1024
ROWS = 256
F32 = jnp.float32
BF16 = jnp.bfloat16


def lanes_low(shape):
    return lax.broadcasted_iota(jnp.int32, shape, len(shape) - 1) % 128 < 64


def merge_half(low, high):
    return jnp.where(lanes_low(low.shape), low, high)


def shifted(value, by):
    row = lax.broadcasted_iota(jnp.int32, value.shape, 0) % 128
    inside = row >= by if by > 0 else row < 128 + by
    return jnp.where(inside, pltpu.roll(value, by % value.shape[0], 0), 0.0)


def build_conv(w_ref, out_ref):
    zero = jnp.zeros((64, 128), BF16)
    for e in range(3):
        for k in range(4):
            for slot, d in enumerate((0, 1, 2, -1)):
                for rx in range(2):
                    a = k - rx
                    halves = []
                    for ry in range(2):
                        b = d - ry + 1
                        live = 0 <= a < 3 and 0 <= b < 3
                        halves.append(w_ref[9 * a + 3 * b + e] if live else zero)
                    row = k * 256 + slot * 64
                    out_ref[e, row : row + 64, rx * 128 : rx * 128 + 128] = merge_half(*halves)


def conv_block(window_ref, slot, par, w_ref):
    lhs = jnp.concatenate([window_ref[slot, 2 * k + par] for k in range(4)], axis=1)
    below, level, above = [jnp.dot(lhs, w_ref[e], preferred_element_type=F32) for e in range(3)]
    return level + shifted(below, 2) + shifted(above, -2)


def gated(ref, plane, index, count):
    inside = (index >= 0) & (index < count)
    block = ref[plane, jnp.clip(index, 0, ref.shape[1] - 1)]
    return jnp.where(inside, block, jnp.zeros_like(block))


def fill_window(window_ref, slot, plane, src_ref, src_plane, index, count):
    window_ref[slot, plane, :, 0:128] = gated(src_ref, src_plane, index, count)
    window_ref[slot, plane, :, 128:256] = merge_half(
        gated(src_ref, src_plane, index + 1, count), gated(src_ref, src_plane, index - 1, count)
    )


def local_kernel(foot_ref, feat_ref, w1_ref, w2_ref, y1_ref, m1_ref, m2_ref, window):
    column = lax.axis_index("bricks") * lax.axis_size("rep") + lax.axis_index("rep")
    count = 2 * foot_ref[1, column]
    build_conv(w1_ref, m1_ref)
    build_conv(w2_ref, m2_ref)

    def fill(t, carry):
        for p in range(8):
            fill_window(window, t, p, feat_ref, p, t, count)
        return carry

    lax.fori_loop(0, count, fill, 0)

    def conv(t, carry):
        for par in range(2):
            out = jnp.maximum(conv_block(window, t, par, m1_ref), 0.0).astype(BF16)
            for rx in range(2):
                y1_ref[2 * rx + par, t] = out[:, 128 * rx : 128 * rx + 128]
        return carry

    lax.fori_loop(0, count, conv, 0)


def main_kernel(
    foot_ref,
    feat_ref,
    halo_ref,
    near_ref,
    m1_ref,
    m2_ref,
    wd_ref,
    wdt_ref,
    head_ref,
    headm_ref,
    label_ref,
    out_ref,
    window,
    hidden,
    hwin,
    down_mat,
    back_mat,
    y2_ref,
    delta_t,
    err_t,
    grad,
    grad_down,
    small,
):
    reps, chans = lax.axis_size("rep"), lax.axis_size("chan")
    columns = lax.axis_size("bricks") * reps
    column = lax.axis_index("bricks") * reps + lax.axis_index("rep")
    planes = BRICK // chans
    mine = lax.axis_index("chan") * planes
    side = mine // 4
    other = column + 2 * side - 1
    present = (other >= 0) & (other < columns)
    other = jnp.clip(other, 0, columns - 1)
    count = 2 * foot_ref[1, column]
    other_count = jnp.where(present, 2 * foot_ref[1, other], 0)
    offset = 2 * (foot_ref[0, other] - foot_ref[0, column])

    grad[...] = jnp.zeros_like(grad)
    grad_down[...] = jnp.zeros_like(grad_down)
    small[...] = jnp.zeros_like(small)
    low = lanes_low((64, 128))
    zero = jnp.zeros((64, 128), BF16)
    for t in range(8):
        ab, e = t // 2, t % 2
        for ry in range(2):
            keep = low if ry == 0 else ~low
            row = ab * 128 + ry * 64
            down_mat[row : row + 64, e * 128 : e * 128 + 128] = jnp.where(keep, wd_ref[t], zero)
            lane = ab * 256 + e * 128
            back_mat[ry * 64 : ry * 64 + 64, lane : lane + 128] = jnp.where(keep, wdt_ref[t], zero)

    def fill(slot, carry):
        t = slot - 1
        for p in range(4):
            fill_window(window, slot, (1 - side) * 4 + p, feat_ref, side * 4 + p, t, count)
            fill_window(window, slot, side * 4 + p, halo_ref, p, t - offset, other_count)
        return carry

    lax.fori_loop(0, count + 2, fill, 0)

    def first(slot, carry):
        t = slot - 1
        own = (t >= 0) & (t < count)
        next_to = (t - offset >= 0) & (t - offset < other_count)
        for par in range(2):
            out = jnp.maximum(conv_block(window, slot, par, m1_ref), 0.0).astype(BF16)
            for rx in range(2):
                live = jnp.where(side == rx, next_to, own)
                block = out[:, 128 * rx : 128 * rx + 128]
                hidden[slot, side * 4 + 2 * rx + par] = jnp.where(
                    live, block, jnp.zeros_like(block)
                )
        for p in range(4):
            hidden[slot, (1 - side) * 4 + p] = gated(near_ref, p, t, count)
        return carry

    lax.fori_loop(0, count + 2, first, 0)

    even = lax.broadcasted_iota(jnp.int32, (128, 128), 0) % 2 == 0
    head_row = head_ref[0:1, :]

    def second(t, carry):
        for p in range(8):
            hwin[p, :, 0:128] = hidden[t + 1, p]
            hwin[p, :, 128:256] = merge_half(hidden[t + 2, p], hidden[t, p])
        for par in range(2):
            lhs = jnp.concatenate([hwin[2 * k + par] for k in range(4)], axis=1)
            below, level, above = [
                jnp.dot(lhs, m2_ref[e], preferred_element_type=F32) for e in range(3)
            ]
            out = level + shifted(below, 2) + shifted(above, -2)
            out = jnp.maximum(out, 0.0).astype(BF16)
            for rx in range(2):
                y2_ref[rx, par] = out[:, 128 * rx : 128 * rx + 128]
        for rx in range(2):
            fine = jnp.concatenate(
                [y2_ref[rx, a, 128 * b : 128 * b + 128] for a in range(2) for b in range(2)], axis=1
            )
            both = jnp.dot(fine, down_mat[...], preferred_element_type=F32)
            coarse = both[:, 0:128] + shifted(both[:, 128:256], -1)
            rect = jnp.maximum(coarse, 0.0)
            logit = jnp.dot(
                rect, headm_ref[...], precision=lax.Precision.HIGHEST, preferred_element_type=F32
            )
            plane = 4 * side + 2 * rx
            keep = even & (plane >= mine) & (plane < mine + planes)
            label = label_ref[2 * side + rx, t].astype(F32)
            tail = jnp.exp(-jnp.abs(logit))
            soft = jnp.maximum(logit, 0.0) + jnp.log1p(tail)
            sigmoid = jnp.where(logit >= 0.0, 1.0, tail) / (1.0 + tail)
            loss = jnp.where(keep, soft - label * logit, 0.0)
            slope = jnp.where(keep, (sigmoid - label) * (1.0 / COARSE), 0.0)
            small[0:1] += jnp.sum(slope * rect, axis=0, keepdims=True)
            small[1:2] += jnp.sum(loss, axis=0, keepdims=True)
            delta = jnp.where(coarse > 0.0, slope * head_row, 0.0).astype(BF16).astype(F32)
            moved = shifted(delta, 1)
            delta_t[0:128, 128 * rx : 128 * rx + 128] = delta.T.astype(BF16)
            delta_t[128:256, 128 * rx : 128 * rx + 128] = moved.T.astype(BF16)
            spread = (delta + moved).astype(BF16)
            back = jnp.dot(spread, back_mat[...], preferred_element_type=F32)
            for a in range(2):
                for b in range(2):
                    lane = (2 * a + b) * 256
                    err = jnp.where(even, back[:, lane : lane + 128], back[:, lane + 128 : lane + 256])
                    live = y2_ref[rx, a, 128 * b : 128 * b + 128].astype(F32) > 0.0
                    err = jnp.where(live, err, 0.0)
                    col = (2 * rx + a) * 256 + b * 128
                    for e, by in enumerate((-2, 0, 2)):
                        value = shifted(err, by) if by else err
                        err_t[128 * e : 128 * e + 128, col : col + 128] = value.T.astype(BF16)
        fine = jnp.concatenate(
            [
                jnp.concatenate([y2_ref[rx, a, 128 * b : 128 * b + 128] for rx in range(2)], axis=0)
                for a in range(2)
                for b in range(2)
            ],
            axis=1,
        )
        grad_down[...] += jnp.dot(delta_t[...], fine, preferred_element_type=F32)
        for a in range(3):
            rows = hwin[2 * a : 2 * a + 4].reshape(4 * ROWS, 256)
            grad[a] += jnp.dot(err_t[...], rows, preferred_element_type=F32)
        return carry

    lax.fori_loop(0, count, second, 0)

    low = lanes_low((64, 128))
    firsts = []
    for a in range(3):
        for e in range(3):
            both = grad[a, 128 * e : 128 * e + 64] + pltpu.roll(
                grad[a, 128 * e + 64 : 128 * e + 128], 192, 1
            )
            out_ref[3 * a + e] = both[:, 0:128]
            firsts.append(both[:, 128:256])
    for m in range(5):
        right = firsts[2 * m + 1] if 2 * m + 1 < 9 else jnp.zeros_like(firsts[0])
        out_ref[9 + m] = jnp.where(low, pltpu.roll(firsts[2 * m], 64, 1), right)
    halves = [
        grad_down[128 * e : 128 * e + 64] + pltpu.roll(grad_down[128 * e + 64 : 128 * e + 128], 448, 1)
        for e in range(2)
    ]
    for ab in range(4):
        tile = jnp.concatenate([half[:, 128 * ab : 128 * ab + 128] for half in halves], axis=0)
        out_ref[14 + ab] = tile.T[0:64]
    sums = small[...]
    head = sums[0:1] + pltpu.roll(sums, 64, 1)[0:1]
    total = jnp.sum(sums[1:2], axis=1, keepdims=True) * (1.0 / 64)
    row = merge_half(head, jnp.broadcast_to(total, (1, 128)))
    out_ref[18] = jnp.broadcast_to(row, (64, 128))


def arrange(features):
    channels, width, rows, depth = features.shape
    split = features.reshape(channels, width, rows // 4, 2, 2, depth)
    return split.transpose(1, 2, 4, 5, 3, 0).reshape(width, rows // 4, 2 * depth, 2 * channels)


def gather_pieces(value, axis):
    peers = lax.axis_size(axis)
    pieces = [value]
    for step in range(1, peers):
        pieces.append(lax.ppermute(value, axis, [(i, (i + step) % peers) for i in range(peers)]))
    order = (lax.axis_index(axis) - jnp.arange(peers)) % peers
    return jnp.stack(pieces)[order]


def gather_weights(w_first, w_second):
    both = jnp.concatenate([w_first, w_second], axis=0)
    taps, channels, share = both.shape
    fold = 128 // share
    packed = both.reshape(taps, fold, channels // fold, share).transpose(0, 2, 1, 3)
    packed = packed.reshape(taps, channels // fold, 128)
    pieces = gather_pieces(packed, "chan")
    pieces = pieces.reshape(-1, taps, channels // fold, fold, share).transpose(1, 3, 2, 0, 4)
    whole = pieces.reshape(taps, channels, -1)
    return jnp.concatenate([whole, whole], axis=2)


def doubling(value, axis):
    peers = lax.axis_size(axis)
    step = 1
    while step < peers:
        value = value + lax.ppermute(value, axis, [(i, i ^ step) for i in range(peers)])
        step *= 2
    return value


def scatter_sum(value, axis, dim):
    peers, me = lax.axis_size(axis), lax.axis_index(axis)
    total = lax.dynamic_index_in_dim(value, me, dim, keepdims=False)
    for step in range(1, peers):
        part = lax.dynamic_index_in_dim(value, (me + step) % peers, dim, keepdims=False)
        total = total + lax.ppermute(part, axis, [(i, (i + step) % peers) for i in range(peers)])
    return total


def shards(features, w_first, w_second, w_down, w_head, footprint, labels):
    bricks, chans, reps = lax.axis_size("bricks"), lax.axis_size("chan"), lax.axis_size("rep")
    planes = BRICK // chans
    side = lax.axis_index("chan") * planes // 4
    features = features[0]
    pairs = []
    for col in range(bricks * reps):
        for c in range(chans):
            src = col + 2 * (c * planes // 4) - 1
            if 0 <= src < bricks * reps:
                ends = [(j // reps * chans + c) * reps + j % reps for j in (src, col)]
                pairs.append(tuple(ends))
    outward = lax.dynamic_slice_in_dim(features, (1 - side) * 4, 4, 1)
    halo = lax.ppermute(outward, ("bricks", "chan", "rep"), pairs)

    weights = gather_weights(w_first, w_second)
    fold = 128 // w_down.shape[2]
    down = gather_pieces(w_down, "chan").transpose(1, 0, 2, 3).reshape(8, -1, w_down.shape[2])
    down2 = jnp.concatenate([down] * fold, axis=2)
    down_t = down.transpose(0, 2, 1)
    down_t2 = jnp.concatenate([down_t] * fold, axis=2)
    head2 = jnp.broadcast_to(jnp.concatenate([w_head, w_head])[None], (8, 128))
    half = jnp.arange(128) // 64
    head_mat = jnp.where(half[:, None] == half[None, :], jnp.concatenate([w_head, w_head])[:, None], 0.0)
    target = labels[0].reshape(4, 6, 2, 64).transpose(0, 1, 3, 2).astype(BF16)
    target = jnp.broadcast_to(target[:, :, :, None, :, None], (4, 6, 64, 2, 2, 64))
    target = target.reshape(4, 6, 128, 128)

    feat = arrange(features)
    slabs = feat.shape[1]
    smem = pl.BlockSpec(memory_space=pltpu.SMEM)
    vmem = pl.BlockSpec(memory_space=pltpu.VMEM)
    near, mat1, mat2 = pl.pallas_call(
        local_kernel,
        out_shape=(
            jax.ShapeDtypeStruct((4, slabs, ROWS, 128), BF16),
            jax.ShapeDtypeStruct((3, 1024, 256), BF16),
            jax.ShapeDtypeStruct((3, 1024, 256), BF16),
        ),
        in_specs=[smem, vmem, vmem, vmem],
        out_specs=(vmem, vmem, vmem),
        scratch_shapes=[pltpu.VMEM((slabs, 8, ROWS, 256), BF16)],
        compiler_params=pltpu.CompilerParams(vmem_limit_bytes=40 << 20),
        cost_estimate=pl.CostEstimate(flops=6 * 6 * 512 * 1024 * 512, bytes_accessed=8 << 20, transcendentals=0),
        name="first_local",
    )(footprint, feat, weights[:27], weights[27:])
    halo = arrange(halo)
    sums = pl.pallas_call(
        main_kernel,
        out_shape=jax.ShapeDtypeStruct((19, 64, 128), F32),
        in_specs=[smem] + [vmem] * 10,
        out_specs=vmem,
        scratch_shapes=[
            pltpu.VMEM((slabs + 2, 8, ROWS, 256), BF16),
            pltpu.VMEM((slabs + 2, 8, ROWS, 128), BF16),
            pltpu.VMEM((8, ROWS, 256), BF16),
            pltpu.VMEM((512, 256), BF16),
            pltpu.VMEM((128, 1024), BF16),
            pltpu.VMEM((2, 2, ROWS, 128), BF16),
            pltpu.VMEM((256, 256), BF16),
            pltpu.VMEM((384, 1024), BF16),
            pltpu.VMEM((3, 384, 256), F32),
            pltpu.VMEM((256, 512), F32),
            pltpu.VMEM((8, 128), F32),
        ],
        compiler_params=pltpu.CompilerParams(vmem_limit_bytes=56 << 20),
        cost_estimate=pl.CostEstimate(flops=4 * 6 * 6 * 512 * 1024 * 512, bytes_accessed=16 << 20, transcendentals=0),
        name="head_and_grads",
    )(footprint, feat, halo, near, mat1, mat2, down2, down_t2, head2, head_mat, target)

    share = 64 // chans
    parts = sums.reshape(19, chans, reps, share // reps, 128)
    mine = scatter_sum(parts, "rep", 2)
    mine = scatter_sum(mine, "chan", 1)
    mine = doubling(mine, "bricks")
    whole = gather_pieces(mine, "rep").transpose(1, 0, 2, 3).reshape(19, share, 128)
    later = whole[:9].reshape(3, 3, share, 2, 64).transpose(0, 3, 1, 4, 2)
    first = whole[9:14].reshape(5, share, 2, 64).transpose(0, 2, 3, 1).reshape(10, 64, share)[:9]
    second = jnp.concatenate([first.reshape(3, 1, 3, 64, share), later], axis=1).reshape(27, 64, share)
    down_out = whole[14:18].reshape(4, share, 2, 64).transpose(0, 2, 1, 3).reshape(8, share, 64)
    live = jnp.sum(footprint[1]).astype(F32)
    loss = (whole[18, 0, 64] / (COARSE * live)).reshape(1)
    return second, down_out, whole[18, 0, :64], loss


def solution(mesh):
    return jax.shard_map(
        shards,
        mesh=mesh,
        in_specs=(
            P(("groups", "bricks", "rep"), None, None, None, None),
            P(None, None, "chan"),
            P(None, None, "chan"),
            P(None, "chan", None),
            P(),
            P(None, "groups"),
            P(("groups", "bricks", "rep"), None, None),
        ),
        out_specs=(P("groups", None, "chan"), P("groups", "chan", None), P("groups"), P("groups")),
        check_vma=False,
    )
```

profile of v0, /device:TPU:0, one launch (start us, length us, event | category | flops | bytes accessed | tf_op | source)
XLA Modules:
  0.0 147.8 jit_solution(7434585692305018104)
XLA Ops:
  0.6 3.0 %collective-permute-start.2 = (bf16[8,32,64]{2,1,0:T(8,128)(2,1)}, bf16[8,32,64]{2,1,0:T(8,128)(2,1)S(1)}, u32[]{:S(2)}, u32[]{:S(2)}) collective-permute-start(bf16[8,32,64]{2,1,0:T(8,128)(2,1)} %param.10), channel_id=1, source_target_pairs={{0,2},{2,0},{1,3},{3,1},{4,6},{6,4},{5,7},{7,5},{8,10},{10,8},{9,1... | collective-permute-start | bytes 98312 | tf_op jit(solution)/shard_map/ppermute | solution.py:272
  3.6 2.6 %copy.114 = bf16[27,64,32]{0,2,1:T(8,128)(2,1)} copy(bf16[27,64,32]{1,2,0:T(8,128)(2,1)} %param.8) | data formatting | bytes 221184 | tf_op args[1]
  6.2 2.7 %copy.115 = bf16[27,64,32]{0,2,1:T(8,128)(2,1)} copy(bf16[27,64,32]{1,2,0:T(8,128)(2,1)} %param.9) | data formatting | bytes 221184 | tf_op args[2]
  8.9 1.5 %pad_maximum_fusion.1 = bf16[54,64,32]{0,2,1:T(8,128)(2,1)S(1)} fusion(bf16[27,64,32]{0,2,1:T(8,128)(2,1)} %copy.115, bf16[27,64,32]{0,2,1:T(8,128)(2,1)} %copy.114), kind=kLoop, calls=%fused_computation.8 | loop fusion | flops 442368 | bytes 442368 | tf_op jit(solution)/shard_map/concatenate | solution.py:278
  10.4 0.8 copy.116
  11.6 1.8 %copy.147 = bf16[1,64,4,24,128]{4,1,3,2,0:T(8,128)(2,1)} copy(bf16[1,64,4,24,128]{4,3,2,1,0:T(8,128)(2,1)S(1)} %constant_dynamic-slice_fusion) | data formatting | bytes 3145728 | tf_op jit(solution)/shard_map/dynamic_slice | solution.py:319
  13.4 2.7 %collective-permute-start = (bf16[64,4,24,128]{3,0,2,1:T(8,128)(2,1)}, bf16[64,4,24,128]{3,0,2,1:T(8,128)(2,1)}, u32[]{:S(2)}, u32[]{:S(2)}) collective-permute-start(bf16[64,4,24,128]{3,0,2,1:T(8,128)(2,1)} %bitcast.67), channel_id=1, source_target_pairs={{3,2},{0,1},{6,3},{1,4},{7,6},{4,5},{10,7},{5,8},{11,10},{8,9},{14... | collective-permute-start | bytes 4718600 | tf_op jit(solution)/shard_map/ppermute | solution.py:320
  16.1 0.7 compare_select_fusion.headm_ref
  17.3 1.3 copy.118
  18.6 1.9 %broadcast_in_dim.19 = bf16[4,6,64,2,2,64]{5,4,3,2,1,0:T(2,128)(2,1)S(1)} broadcast(bf16[4,6,64,2]{3,2,1,0:T(8,128)(2,1)S(1)} %copy.127), dimensions={0,1,2,4} | broadcast | bytes 792576 | tf_op jit(solution)/shard_map/broadcast_in_dim | solution.py:332
  20.5 1.5 %reshape.208.label_ref = bf16[4,6,128,128]{3,2,1,0:T(8,128)(2,1)} reshape(bf16[4,6,64,2,2,64]{5,4,3,2,1,0:T(2,128)(2,1)S(1)} %broadcast_in_dim.19) | data formatting | bytes 1572864 | tf_op jit(solution)/shard_map/reshape | solution.py:333
  22.0 5.4 %copy.146 = bf16[64,8,6,2,2,128]{5,4,0,3,2,1:T(2,128)(2,1)S(1)} copy(bf16[64,8,6,2,2,128]{5,4,3,2,1,0:T(2,128)(2,1)} %bitcast.69) | data formatting | bytes 6291456 | tf_op jit(solution)/shard_map/reshape;squeeze | solution.py:264
  27.4 3.8 %reshape.200 = bf16[8,6,256,128]{2,3,1,0:T(8,128)(2,1)} reshape(bf16[8,6,2,128,2,64]{3,2,5,4,1,0:T(2,128)(2,1)S(1)} %bitcast.68) | data formatting | bytes 6291456 | tf_op jit(solution)/shard_map/reshape | solution.py:265
  31.2 3.5 %copy.128.feat_ref = bf16[8,6,256,128]{3,2,1,0:T(8,128)(2,1)S(1)} copy(bf16[8,6,256,128]{2,3,1,0:T(8,128)(2,1)} %reshape.200) | data formatting | bytes 6291456 | tf_op jit(solution)/shard_map/reshape | solution.py:265
  34.7 0.7 copy-done.7
  35.4 1.1 pad_maximum_fusion.5
  36.4 1.2 gather_fusion.1
  37.7 0.9 copy.125
  38.6 0.8 copy.126
  39.4 1.8 %pad_maximum_fusion.6 = (bf16[8,64,128]{2,1,0:T(8,128)(2,1)}, bf16[8,64,128]{2,1,0:T(8,128)(2,1)}) fusion(bf16[8,64,64]{2,1,0:T(8,128)(2,1)S(1)} %bitcast.79, bf16[8,64,64]{2,1,0:T(8,128)(2,1)} %bitcast.88), kind=kLoop, calls=%fused_computation.18 | loop fusion | flops 524288 | bytes 393216 | tf_op jit(solution)/shard_map/concatenate | solution.py:325
  41.2 2.0 %copy.119 = bf16[1,54,16,128]{3,2,1,0:T(8,128)(2,1)} copy(bf16[1,54,16,128]{1,3,2,0:T(8,128)(2,1)} %bitcast.9) | data formatting | bytes 442368 | tf_op jit(solution)/shard_map/stack | solution.py:274
  43.2 1.7 %pad_maximum_fusion.3 = bf16[2,54,16,128]{3,2,1,0:T(8,128)(2,1)} fusion(bf16[1,54,16,128]{3,2,1,0:T(8,128)(2,1)} %copy.119, bf16[1,54,16,128]{3,2,1,0:T(8,128)(2,1)S(1)} %copy.118), kind=kLoop, calls=%fused_computation.11 | loop fusion | flops 221184 | bytes 884736 | tf_op jit(solution)/shard_map/stack | solution.py:274
  45.0 2.4 %gather_fusion = bf16[2,54,16,128]{3,2,1,0:T(8,128)(2,1)} fusion(bf16[2,54,16,128]{3,2,1,0:T(8,128)(2,1)} %pad_maximum_fusion.3, s32[1024]{0:T(1024)S(1)} %pad_clamp_fusion.1), kind=kCustom, calls=%fused_computation | custom fusion | bytes 884744 | tf_op jit(solution)/shard_map/gather | solution.py:274
  47.3 2.5 %copy.120 = bf16[2,54,16,128]{1,3,2,0:T(8,128)(2,1)} copy(bf16[2,54,16,128]{3,2,1,0:T(8,128)(2,1)} %gather_fusion) | data formatting | bytes 884736 | tf_op jit(solution)/shard_map/gather | solution.py:274
  49.8 2.4 %copy.121 = bf16[54,4,16,2,32]{0,4,3,2,1:T(8,128)(2,1)} copy(bf16[54,4,16,2,32]{0,4,1,2,3:T(8,128)(2,1)} %bitcast.70) | data formatting | bytes 884736 | tf_op jit(solution)/shard_map/transpose | solution.py:284
  52.2 3.2 %copy.122 = bf16[54,64,64]{2,1,0:T(8,128)(2,1)} copy(bf16[54,64,64]{0,2,1:T(8,128)(2,1)} %bitcast.71) | data formatting | bytes 884736 | tf_op jit(solution)/shard_map/reshape | solution.py:285
  55.5 2.0 %pad_maximum_fusion.2 = (bf16[27,64,128]{2,1,0:T(8,128)(2,1)S(1)}, bf16[27,64,128]{2,1,0:T(8,128)(2,1)S(1)}) fusion(bf16[54,64,64]{2,1,0:T(8,128)(2,1)} %copy.122), kind=kLoop, calls=%fused_computation.10 | loop fusion | flops 1769472 | bytes 1327104 | tf_op jit(solution)/shard_map/concatenate | solution.py:286
  57.5 3.8 %first_local.1 = (bf16[4,6,256,128]{3,2,1,0:T(8,128)(2,1)S(1)}, bf16[3,1024,256]{2,1,0:T(8,128)(2,1)S(1)}, bf16[3,1024,256]{2,1,0:T(8,128)(2,1)S(1)}) custom-call(s32[2,8]{1,0:T(2,128)S(1)} %copy-done.1, bf16[8,6,256,128]{3,2,1,0:T(8,128)(2,1)S(1)} %copy.128.feat_ref, bf16[27,64,128]{2,1,0:T(8,128)(2,1)S(1)} %get-tuple-element.11.w1_ref, ...), custom_call_target="tpu_custom_call" | custom-call | flops 9663676416 | bytes 8388608 | tf_op jit(solution)/shard_map/first_local/pallas_call | solution.py:339
  61.3 1.1 copy-done.3
  62.4 1.2 copy-done.4
  63.6 1.1 copy-done.5
  64.8 6.7 %copy.140 = bf16[4,6,2,128,2,64]{5,4,3,2,1,0:T(2,128)(2,1)S(1)} copy(bf16[4,6,2,128,2,64]{3,5,2,4,1,0:T(8,128)(2,1)} %bitcast.4) | data formatting | bytes 3145728 | tf_op jit(solution)/shard_map/reshape | solution.py:265
  71.5 2.6 %reshape.243.halo_ref = bf16[4,6,256,128]{3,2,1,0:T(8,128)(2,1)} reshape(bf16[4,6,2,128,2,64]{5,4,3,2,1,0:T(2,128)(2,1)S(1)} %copy.140) | data formatting | bytes 3145728 | tf_op jit(solution)/shard_map/reshape | solution.py:265
  74.1 0.6 broadcast_in_dim.12.head_ref
  74.7 17.1 %head_and_grads.1 = f32[19,64,128]{2,1,0:T(8,128)} custom-call(s32[2,8]{1,0:T(2,128)} %foot_ref.3, bf16[8,6,256,128]{3,2,1,0:T(8,128)(2,1)} %copy-done, bf16[4,6,256,128]{3,2,1,0:T(8,128)(2,1)} %reshape.243.halo_ref, bf16[4,6,256,128]{3,2,1,0:T(8,128)(2,1)} %copy-done.3, bf16[3,1024,256]{2,1,0:T(8,128)(2,1)} %copy-done.4, bf16[3,1024,256]{2,1,0:T(8,128)(2,1)} %copy-done.5, ...), custom_call_target="tpu_custom_call" | custom-call | flops 38654705664 | bytes 16777216 | tf_op jit(solution)/shard_map/head_and_grads/pallas_call | solution.py:354
  91.9 1.0 dynamic-slice_bitcast_fusion
  92.9 24.3 %collective-permute-start.3 = (f32[19,2,16,128]{3,2,1,0:T(8,128)S(1)}, f32[19,2,16,128]{3,2,1,0:T(8,128)S(1)}, u32[]{:S(2)}, u32[]{:S(2)}) collective-permute-start(f32[19,2,16,128]{3,2,1,0:T(8,128)S(1)} %dynamic-slice_bitcast_fusion), channel_id=1, source_target_pairs={{0,1},{1,0},{2,3},{3,2},{4,5},{5,4},{6,7},{7,6},{8,9},{9,8},{10,11... | collective-permute-start | bytes 933896 | tf_op jit(solution)/shard_map/ppermute | solution.py:303
  117.2 1.2 collective-permute-done.3
  118.4 1.0 bitcast_add_fusion
  119.9 6.0 %collective-permute-done.4 = f32[19,16,128]{2,1,0:T(8,128)S(1)} collective-permute-done((f32[19,16,128]{2,1,0:T(8,128)S(1)}, f32[19,16,128]{2,1,0:T(8,128)S(1)}, u32[]{:S(2)}, u32[]{:S(2)}) %collective-permute-start.4) | collective-permute-done | bytes 155680 | tf_op jit(solution)/shard_map/ppermute | solution.py:303
  125.9 1.6 %collective-permute-start.5 = (f32[19,16,128]{2,1,0:T(8,128)S(1)}, f32[19,16,128]{2,1,0:T(8,128)S(1)}, u32[]{:S(2)}, u32[]{:S(2)}) collective-permute-start(f32[19,16,128]{2,1,0:T(8,128)S(1)} %bitcast_add_fusion.1), channel_id=1, source_target_pairs={{0,4},{4,0},{8,12},{12,8},{1,5},{5,1},{9,13},{13,9},{2,6},{6,2},{1... | collective-permute-start | bytes 466952 | tf_op jit(solution)/shard_map/ppermute | solution.py:293
  127.5 3.9 %collective-permute-done.5 = f32[19,16,128]{2,1,0:T(8,128)S(1)} collective-permute-done((f32[19,16,128]{2,1,0:T(8,128)S(1)}, f32[19,16,128]{2,1,0:T(8,128)S(1)}, u32[]{:S(2)}, u32[]{:S(2)}) %collective-permute-start.5) | collective-permute-done | bytes 155680 | tf_op jit(solution)/shard_map/ppermute | solution.py:293
  131.5 2.6 %collective-permute-start.6 = (f32[19,16,128]{2,1,0:T(8,128)S(1)}, f32[19,16,128]{2,1,0:T(8,128)S(1)}, u32[]{:S(2)}, u32[]{:S(2)}) collective-permute-start(f32[19,16,128]{2,1,0:T(8,128)S(1)} %add.112), channel_id=1, source_target_pairs={{0,8},{4,12},{8,0},{12,4},{1,9},{5,13},{9,1},{13,5},{2,10},{6,14},... | collective-permute-start | bytes 466952 | tf_op jit(solution)/shard_map/ppermute | solution.py:293
  134.1 0.6 slice_reduce_fusion
  134.7 5.6 %collective-permute-done.6 = f32[19,16,128]{2,1,0:T(8,128)S(1)} collective-permute-done((f32[19,16,128]{2,1,0:T(8,128)S(1)}, f32[19,16,128]{2,1,0:T(8,128)S(1)}, u32[]{:S(2)}, u32[]{:S(2)}) %collective-permute-start.6) | collective-permute-done | bytes 155680 | tf_op jit(solution)/shard_map/ppermute | solution.py:293
  141.1 0.7 collective-permute-done.7
  143.7 0.7 copy.138
  145.2 0.8 copy.136
  (53 shorter events, 4.0 us)
Async XLA Ops:
  0.6 34.1 %collective-permute-start.2 = (bf16[8,32,64]{2,1,0:T(8,128)(2,1)}, bf16[8,32,64]{2,1,0:T(8,128)(2,1)S(1)}, u32[]{:S(2)}, u32[]{:S(2)}) collective-permute-start(bf16[8,32,64]{2,1,0:T(8,128)(2,1)} %param.10), channel_id=1, source_target_pairs={{0,2},{2,0},{1,3},{3,1},{4,6},{6,4},{5,7},{7,5},{8,10},{10,8},{9,1... | collective-permute-start | bytes 98312 | tf_op jit(solution)/shard_map/ppermute | solution.py:272
  6.2 5.1 %copy-start.6 = (bf16[1,64,8,24,128]{4,3,2,1,0:T(8,128)(2,1)S(1)}, bf16[1,64,8,24,128]{4,3,2,1,0:T(8,128)(2,1)}, u32[]{:S(2)}) copy-start(bf16[1,64,8,24,128]{4,3,2,1,0:T(8,128)(2,1)} %param.7) | copy-start | bytes 9437188
  11.3 29.9 %collective-permute-start.1 = (bf16[54,16,128]{0,2,1:T(8,128)(2,1)}, bf16[54,16,128]{0,2,1:T(8,128)(2,1)}, u32[]{:S(2)}, u32[]{:S(2)}) collective-permute-start(bf16[54,16,128]{0,2,1:T(8,128)(2,1)} %bitcast.8), channel_id=1, source_target_pairs={{0,2},{2,0},{1,3},{3,1},{4,6},{6,4},{5,7},{7,5},{8,10},{10,8},{9,1... | collective-permute-start | bytes 663560 | tf_op jit(solution)/shard_map/ppermute | solution.py:272
  11.6 4.5 %copy-start.9 = (f32[64]{0:T(128)S(1)}, f32[64]{0:T(128)}, u32[]{:S(2)}) copy-start(f32[64]{0:T(128)} %param.11) | copy-start | bytes 772
  11.6 5.3 %copy-start.8 = (s32[1,4,768]{2,1,0:T(4,128)S(1)}, s32[1,4,768]{2,1,0:T(4,128)}, u32[]{:S(2)}) copy-start(s32[1,4,768]{2,1,0:T(4,128)} %param.13) | copy-start | bytes 36868
  13.4 51.4 %collective-permute-start = (bf16[64,4,24,128]{3,0,2,1:T(8,128)(2,1)}, bf16[64,4,24,128]{3,0,2,1:T(8,128)(2,1)}, u32[]{:S(2)}, u32[]{:S(2)}) collective-permute-start(bf16[64,4,24,128]{3,0,2,1:T(8,128)(2,1)} %bitcast.67), channel_id=1, source_target_pairs={{3,2},{0,1},{6,3},{1,4},{7,6},{4,5},{10,7},{5,8},{11,10},{8,9},{14... | collective-permute-start | bytes 4718600 | tf_op jit(solution)/shard_map/ppermute | solution.py:320
  34.7 22.8 %copy-start = (bf16[8,6,256,128]{3,2,1,0:T(8,128)(2,1)}, bf16[8,6,256,128]{3,2,1,0:T(8,128)(2,1)S(1)}, u32[]{:S(2)}) copy-start(bf16[8,6,256,128]{3,2,1,0:T(8,128)(2,1)S(1)} %copy.128.feat_ref) | copy-start | bytes 9437188
  34.7 0.7 copy-start.7
  52.2 5.2 %copy-start.1 = (s32[2,8]{1,0:T(2,128)S(1)}, s32[2,8]{1,0:T(2,128)}, u32[]{:S(2)}) copy-start(s32[2,8]{1,0:T(2,128)} %foot_ref.3) | copy-start | bytes 196
  61.2 1.2 copy-start.3
  62.4 1.2 copy-start.4
  63.6 1.1 copy-start.5
  91.9 42.2 %copy-start.2 = (s32[2,8]{1,0:T(2,128)S(1)}, s32[2,8]{1,0:T(2,128)}, u32[]{:S(2)}) copy-start(s32[2,8]{1,0:T(2,128)} %foot_ref.3) | copy-start | bytes 196
  92.9 25.6 %collective-permute-start.3 = (f32[19,2,16,128]{3,2,1,0:T(8,128)S(1)}, f32[19,2,16,128]{3,2,1,0:T(8,128)S(1)}, u32[]{:S(2)}, u32[]{:S(2)}) collective-permute-start(f32[19,2,16,128]{3,2,1,0:T(8,128)S(1)} %dynamic-slice_bitcast_fusion), channel_id=1, source_target_pairs={{0,1},{1,0},{2,3},{3,2},{4,5},{5,4},{6,7},{7,6},{8,9},{9,8},{10,11... | collective-permute-start | bytes 933896 | tf_op jit(solution)/shard_map/ppermute | solution.py:303
  119.5 6.4 %collective-permute-start.4 = (f32[19,16,128]{2,1,0:T(8,128)S(1)}, f32[19,16,128]{2,1,0:T(8,128)S(1)}, u32[]{:S(2)}, u32[]{:S(2)}) collective-permute-start(f32[19,16,128]{2,1,0:T(8,128)S(1)} %dynamic-slice_bitcast_fusion.1), channel_id=1, source_target_pairs={{0,2},{2,0},{1,3},{3,1},{4,6},{6,4},{5,7},{7,5},{8,10},{10,8},{9,1... | collective-permute-start | bytes 466952 | tf_op jit(solution)/shard_map/ppermute | solution.py:303
  125.9 5.5 %collective-permute-start.5 = (f32[19,16,128]{2,1,0:T(8,128)S(1)}, f32[19,16,128]{2,1,0:T(8,128)S(1)}, u32[]{:S(2)}, u32[]{:S(2)}) collective-permute-start(f32[19,16,128]{2,1,0:T(8,128)S(1)} %bitcast_add_fusion.1), channel_id=1, source_target_pairs={{0,4},{4,0},{8,12},{12,8},{1,5},{5,1},{9,13},{13,9},{2,6},{6,2},{1... | collective-permute-start | bytes 466952 | tf_op jit(solution)/shard_map/ppermute | solution.py:293
  131.5 8.9 %collective-permute-start.6 = (f32[19,16,128]{2,1,0:T(8,128)S(1)}, f32[19,16,128]{2,1,0:T(8,128)S(1)}, u32[]{:S(2)}, u32[]{:S(2)}) collective-permute-start(f32[19,16,128]{2,1,0:T(8,128)S(1)} %add.112), channel_id=1, source_target_pairs={{0,8},{4,12},{8,0},{12,4},{1,9},{5,13},{9,1},{13,5},{2,10},{6,14},... | collective-permute-start | bytes 466952 | tf_op jit(solution)/shard_map/ppermute | solution.py:293
  140.3 1.4 collective-permute-start.7
where the time goes:
time: 149 us; the launch traced here: 148 us
  local copies, waits for them, and re-layouts  60.3 us (40%)
  starting transfers between devices  34.8 us (23%)
  Pallas kernels  20.9 us (14%)
  waiting for transfers between devices  17.4 us (12%)
  other arithmetic  11 us (7%)
  between operations  3.39 us (2%)
    ppermute x2, starting transfers between devices, scatter_sum(): lax.ppermute(part, axis, [(i, (i + step) % peers) for i in range(peers)])  24.7 us
    pallas_call x1, Pallas kernels, shards(): pl.pallas_call(main_kernel, out_shape=jax.ShapeDtypeStruct((19, 64, 128),...  17.1 us
    reshape x4, local copies, waits for them, and re-layouts, arrange(): split.transpose(1, 2, 4, 5, 3, 0)  16.6 us
    unnamed x22, local copies, waits for them, and re-layouts  9.52 us
    ppermute x2, waiting for transfers between devices, doubling(): lax.ppermute(value, axis, [(i, i ^ step) for i in range(peers)])  9.5 us
    ppermute x2, waiting for transfers between devices, scatter_sum(): lax.ppermute(part, axis, [(i, (i + step) % peers) for i in range(peers)])  7.21 us
    gather x4, local copies, waits for them, and re-layouts, gather_pieces(): return jnp.stack(pieces)[order]  6.66 us
    another operation x1, local copies, waits for them, and re-layouts, arrange(): split = features.reshape(channels, width, rows // 4, 2, 2, depth)  5.42 us
  transfers between devices with their start and end apart: 8, of which 5 were waited for; matrix products, arithmetic and copies ran while one was open for 34% of the time, Pallas kernels for 3%

commit v1 on v0

v1 whole, which is shorter than its diff:
```python
import jax
import jax.numpy as jnp
from jax import lax
from jax.experimental import pallas as pl
from jax.experimental.pallas import tpu as pltpu
from jax.sharding import PartitionSpec as P

BRICK = 8
COARSE = 1024
ROWS = 256
F32 = jnp.float32
BF16 = jnp.bfloat16


def lanes_low(shape):
    return lax.broadcasted_iota(jnp.int32, shape, len(shape) - 1) % 128 < 64


def merge_half(low, high):
    return jnp.where(lanes_low(low.shape), low, high)


def shifted(value, by):
    row = lax.broadcasted_iota(jnp.int32, value.shape, 0) % 128
    inside = row >= by if by > 0 else row < 128 + by
    return jnp.where(inside, pltpu.roll(value, by % value.shape[0], 0), 0.0)


def build_conv(w_ref, out_ref):
    zero = jnp.zeros((64, 128), BF16)
    for e in range(3):
        for k in range(4):
            for slot, d in enumerate((0, 1, 2, -1)):
                for rx in range(2):
                    a = k - rx
                    halves = []
                    for ry in range(2):
                        b = d - ry + 1
                        live = 0 <= a < 3 and 0 <= b < 3
                        halves.append(w_ref[9 * a + 3 * b + e] if live else zero)
                    row = k * 256 + slot * 64
                    out_ref[e, row : row + 64, rx * 128 : rx * 128 + 128] = merge_half(*halves)


def conv_block(window_ref, slot, par, w_ref):
    lhs = jnp.concatenate([window_ref[slot, 2 * k + par] for k in range(4)], axis=1)
    below, level, above = [jnp.dot(lhs, w_ref[e], preferred_element_type=F32) for e in range(3)]
    return level + shifted(below, 2) + shifted(above, -2)


def gated(ref, plane, index, count):
    inside = (index >= 0) & (index < count)
    block = ref[plane, jnp.clip(index, 0, ref.shape[1] - 1)]
    return jnp.where(inside, block, jnp.zeros_like(block))


def turn_block(src_ref, dst_ref, plane, t):
    for py in range(2):
        tall = jnp.concatenate([src_ref[plane, 4 * t + py], src_ref[plane, 4 * t + 2 + py]], axis=0)
        dst_ref[plane, t, 128 * py : 128 * py + 128] = tall.T


def fill_window(window_ref, slot, plane, src_ref, src_plane, index, count):
    window_ref[slot, plane, :, 0:128] = gated(src_ref, src_plane, index, count)
    window_ref[slot, plane, :, 128:256] = merge_half(
        gated(src_ref, src_plane, index + 1, count), gated(src_ref, src_plane, index - 1, count)
    )


def pack_kernel(w1_ref, w2_ref, wd_ref, out_ref):
    half = w1_ref.shape[1] // 2
    start = 0
    for ref in (w1_ref, w2_ref, wd_ref):
        stop = start + ref.shape[0]
        out_ref[start:stop] = jnp.concatenate([ref[:, :half], ref[:, half:]], axis=2)
        start = stop


def local_kernel(foot_ref, feat_ref, *refs):
    chans = lax.axis_size("chan")
    piece_refs = refs[:chans]
    edge_ref, y1_ref, m1_ref, m2_ref, down_ref, back_ref, whole, turned, arranged, window = refs[chans:]
    column = lax.axis_index("bricks") * lax.axis_size("rep") + lax.axis_index("rep")
    me = lax.axis_index("chan")
    side = me * (BRICK // chans) // 4
    count = 2 * foot_ref[1, column]

    half = piece_refs[0].shape[1]
    for step in range(chans):
        block = piece_refs[step][...]
        source = lax.rem(me - step + chans, chans)
        for h in range(2):
            part = block[:, :, 64 * h : 64 * h + 64]
            rows = pl.ds(pl.multiple_of((2 * source + h) * half, half), half)
            whole[:, rows, :] = jnp.concatenate([part, part], axis=2)
    for t in range(54):
        turned[t] = jnp.concatenate([whole[t], whole[t]], axis=0).T[0:64]
    build_conv(turned.at[0:27], m1_ref)
    build_conv(turned.at[27:54], m2_ref)
    low = lanes_low((64, 128))
    zero = jnp.zeros((64, 128), BF16)
    for t in range(8):
        ab, e = t // 2, t % 2
        block = whole[54 + t]
        tile = jnp.concatenate([jnp.where(low, block, zero), jnp.where(low, zero, block)], axis=0)
        down_ref[ab * 128 : ab * 128 + 128, e * 128 : e * 128 + 128] = tile
        back_ref[:, t * 128 : t * 128 + 128] = tile.T

    def turn(t, carry):
        for p in range(8):
            turn_block(feat_ref, arranged, p, t)
        for p in range(4):
            edge_ref[p, t] = arranged[4 * side + p, t]
        return carry

    lax.fori_loop(0, count, turn, 0)

    def fill(t, carry):
        for p in range(8):
            fill_window(window, t, p, arranged, p, t, count)
        return carry

    lax.fori_loop(0, count, fill, 0)

    def conv(t, carry):
        for par in range(2):
            out = jnp.maximum(conv_block(window, t, par, m1_ref), 0.0).astype(BF16)
            for rx in range(2):
                y1_ref[2 * rx + par, t] = out[:, 128 * rx : 128 * rx + 128]
        return carry

    lax.fori_loop(0, count, conv, 0)


def main_kernel(
    foot_ref,
    edge_ref,
    halo_ref,
    near_ref,
    m1_ref,
    m2_ref,
    down_mat,
    back_mat,
    head_ref,
    label_ref,
    keep_ref,
    send_ref,
    arranged,
    window,
    hidden,
    hwin,
    headm_ref,
    y2_ref,
    delta_t,
    err_t,
    grad,
    grad_down,
    small,
):
    reps, chans = lax.axis_size("rep"), lax.axis_size("chan")
    columns = lax.axis_size("bricks") * reps
    column = lax.axis_index("bricks") * reps + lax.axis_index("rep")
    planes = BRICK // chans
    mine = lax.axis_index("chan") * planes
    side = mine // 4
    other = column + 2 * side - 1
    present = (other >= 0) & (other < columns)
    other = jnp.clip(other, 0, columns - 1)
    count = 2 * foot_ref[1, column]
    other_count = jnp.where(present, 2 * foot_ref[1, other], 0)
    offset = 2 * (foot_ref[0, other] - foot_ref[0, column])

    grad[...] = jnp.zeros_like(grad)
    grad_down[...] = jnp.zeros_like(grad_down)
    small[...] = jnp.zeros_like(small)
    head_row = jnp.concatenate([head_ref[...], head_ref[...]], axis=1)
    square_row = lax.broadcasted_iota(jnp.int32, (128, 128), 0)
    square_lane = lax.broadcasted_iota(jnp.int32, (128, 128), 1)
    same_half = (square_row < 64) == (square_lane < 64)
    headm_ref[...] = jnp.where(same_half, jnp.broadcast_to(head_row, (128, 128)).T, 0.0)
    pick_depth = jnp.where(square_row // 2 == square_lane % 64, 1.0, 0.0).astype(BF16)

    def turn(t, carry):
        for p in range(4):
            turn_block(halo_ref, arranged, p, t)
        return carry

    lax.fori_loop(0, other_count, turn, 0)

    def fill(slot, carry):
        t = slot - 1
        for p in range(4):
            fill_window(window, slot, (1 - side) * 4 + p, edge_ref, p, t, count)
            fill_window(window, slot, side * 4 + p, arranged, p, t - offset, other_count)
        return carry

    lax.fori_loop(0, count + 2, fill, 0)

    def first(slot, carry):
        t = slot - 1
        own = (t >= 0) & (t < count)
        next_to = (t - offset >= 0) & (t - offset < other_count)
        for par in range(2):
            out = jnp.maximum(conv_block(window, slot, par, m1_ref), 0.0).astype(BF16)
            for rx in range(2):
                live = jnp.where(side == rx, next_to, own)
                block = out[:, 128 * rx : 128 * rx + 128]
                hidden[slot, side * 4 + 2 * rx + par] = jnp.where(
                    live, block, jnp.zeros_like(block)
                )
        for p in range(4):
            hidden[slot, (1 - side) * 4 + p] = gated(near_ref, p, t, count)
        return carry

    lax.fori_loop(0, count + 2, first, 0)

    even = square_row % 2 == 0

    def second(t, carry):
        for p in range(8):
            hwin[p, :, 0:128] = hidden[t + 1, p]
            hwin[p, :, 128:256] = merge_half(hidden[t + 2, p], hidden[t, p])
        for par in range(2):
            lhs = jnp.concatenate([hwin[2 * k + par] for k in range(4)], axis=1)
            below, level, above = [
                jnp.dot(lhs, m2_ref[e], preferred_element_type=F32) for e in range(3)
            ]
            out = level + shifted(below, 2) + shifted(above, -2)
            out = jnp.maximum(out, 0.0).astype(BF16)
            for rx in range(2):
                y2_ref[rx, par] = out[:, 128 * rx : 128 * rx + 128]
        for rx in range(2):
            fine = jnp.concatenate(
                [y2_ref[rx, a, 128 * b : 128 * b + 128] for a in range(2) for b in range(2)], axis=1
            )
            both = jnp.dot(fine, down_mat[...], preferred_element_type=F32)
            coarse = both[:, 0:128] + shifted(both[:, 128:256], -1)
            rect = jnp.maximum(coarse, 0.0)
            logit = jnp.dot(
                rect, headm_ref[...], precision=lax.Precision.HIGHEST, preferred_element_type=F32
            )
            plane = 4 * side + 2 * rx
            keep = even & (plane >= mine) & (plane < mine + planes)
            line = label_ref[:, pl.ds(pl.multiple_of(128 * t, 128), 128)].astype(F32)
            row = jnp.where(side == 1, line[2 + rx : 3 + rx], line[rx : rx + 1])
            row = jnp.broadcast_to(row, (128, 128))
            row = jnp.where(same_half, row, 0.0).astype(BF16)
            label = lax.dot_general(
                pick_depth, row, (((1,), (1,)), ((), ())), preferred_element_type=F32
            )
            tail = jnp.exp(-jnp.abs(logit))
            soft = jnp.maximum(logit, 0.0) + jnp.log1p(tail)
            sigmoid = jnp.where(logit >= 0.0, 1.0, tail) / (1.0 + tail)
            loss = jnp.where(keep, soft - label * logit, 0.0)
            slope = jnp.where(keep, (sigmoid - label) * (1.0 / COARSE), 0.0)
            small[0:1] += jnp.sum(slope * rect, axis=0, keepdims=True)
            small[1:2] += jnp.sum(loss, axis=0, keepdims=True)
            delta = jnp.where(coarse > 0.0, slope * head_row, 0.0).astype(BF16).astype(F32)
            moved = shifted(delta, 1)
            delta_t[0:128, 128 * rx : 128 * rx + 128] = delta.T.astype(BF16)
            delta_t[128:256, 128 * rx : 128 * rx + 128] = moved.T.astype(BF16)
            spread = (delta + moved).astype(BF16)
            back = jnp.dot(spread, back_mat[...], preferred_element_type=F32)
            for a in range(2):
                for b in range(2):
                    lane = (2 * a + b) * 256
                    err = jnp.where(even, back[:, lane : lane + 128], back[:, lane + 128 : lane + 256])
                    live = y2_ref[rx, a, 128 * b : 128 * b + 128].astype(F32) > 0.0
                    err = jnp.where(live, err, 0.0)
                    col = (2 * rx + a) * 256 + b * 128
                    turned = err.astype(BF16).T.astype(F32)
                    up = jnp.where(square_lane < 126, pltpu.roll(turned, 126, 1), 0.0)
                    down = jnp.where(square_lane >= 2, pltpu.roll(turned, 2, 1), 0.0)
                    for e, value in enumerate((up, turned, down)):
                        err_t[128 * e : 128 * e + 128, col : col + 128] = value.astype(BF16)
        fine = jnp.concatenate(
            [
                jnp.concatenate([y2_ref[rx, a, 128 * b : 128 * b + 128] for rx in range(2)], axis=0)
                for a in range(2)
                for b in range(2)
            ],
            axis=1,
        )
        grad_down[...] += jnp.dot(delta_t[...], fine, preferred_element_type=F32)
        for a in range(3):
            rows = hwin[2 * a : 2 * a + 4].reshape(4 * ROWS, 256)
            grad[a] += jnp.dot(err_t[...], rows, preferred_element_type=F32)
        return carry

    lax.fori_loop(0, count, second, 0)

    low = lanes_low((64, 128))
    rep, chan = lax.axis_index("rep"), lax.axis_index("chan")
    share = 64 // chans // reps

    def emit(slab, value):
        for c in range(chans):
            place = lax.rem(c - chan + chans, chans)
            for r in range(reps):
                rows = value[(c * reps + r) * share : (c * reps + r + 1) * share]

                @pl.when(rep == r)
                def _():
                    keep_ref[place, slab] = rows

                @pl.when(rep != r)
                def _():
                    send_ref[place, slab] = rows

    firsts = []
    for a in range(3):
        for e in range(3):
            both = grad[a, 128 * e : 128 * e + 64] + pltpu.roll(
                grad[a, 128 * e + 64 : 128 * e + 128], 192, 1
            )
            emit(3 * a + e, both[:, 0:128])
            firsts.append(both[:, 128:256])
    for m in range(5):
        right = firsts[2 * m + 1] if 2 * m + 1 < 9 else jnp.zeros_like(firsts[0])
        emit(9 + m, jnp.where(low, pltpu.roll(firsts[2 * m], 64, 1), right))
    halves = [
        grad_down[128 * e : 128 * e + 64] + pltpu.roll(grad_down[128 * e + 64 : 128 * e + 128], 448, 1)
        for e in range(2)
    ]
    for ab in range(4):
        tile = jnp.concatenate([half[:, 128 * ab : 128 * ab + 128] for half in halves], axis=0)
        emit(14 + ab, tile.T[0:64])
    sums = small[...]
    head = sums[0:1] + pltpu.roll(sums, 64, 1)[0:1]
    total = jnp.sum(sums[1:2], axis=1, keepdims=True) * (1.0 / 64)
    row = merge_half(head, jnp.broadcast_to(total, (1, 128)))
    emit(18, jnp.broadcast_to(row, (64, 128)))


def final_kernel(foot_ref, mine_ref, peer_ref, second_ref, down_ref, head_ref, loss_ref):
    rep = lax.axis_index("rep")
    share = mine_ref.shape[1]
    for ref, r in ((mine_ref, rep), (peer_ref, 1 - rep)):
        rows = pl.ds(pl.multiple_of(r * share, share), share)
        for a in range(3):
            for e in range(3):
                m = 3 * a + e
                later, first = ref[m], ref[9 + m // 2]
                second_ref[9 * a + e, rows] = first[:, 64 * (m % 2) : 64 * (m % 2) + 64]
                second_ref[9 * a + 3 + e, rows] = later[:, 0:64]
                second_ref[9 * a + 6 + e, rows] = later[:, 64:128]
        for ab in range(4):
            for e in range(2):
                down_ref[2 * ab + e, rows] = ref[14 + ab][:, 64 * e : 64 * e + 64]
    line = mine_ref[18][0:1]
    head_ref[...] = line[:, 0:64]
    live = foot_ref[1, 0]
    for c in range(1, foot_ref.shape[1]):
        live += foot_ref[1, c]
    scale = jnp.full((1, 1), COARSE * live, jnp.int32).astype(F32)
    loss_ref[...] = line[:, 64:65] / scale


def shards(features, w_first, w_second, w_down, w_head, footprint, labels):
    bricks, chans, reps = lax.axis_size("bricks"), lax.axis_size("chan"), lax.axis_size("rep")
    planes = BRICK // chans
    side = lax.axis_index("chan") * planes // 4
    smem = pl.BlockSpec(memory_space=pltpu.SMEM)
    vmem = pl.BlockSpec(memory_space=pltpu.VMEM)
    features = features[0]
    slabs = features.shape[2] // 4

    packed = pl.pallas_call(
        pack_kernel,
        out_shape=jax.ShapeDtypeStruct((62, 32 // chans, 128), BF16),
        in_specs=[vmem] * 3,
        out_specs=vmem,
        name="pack",
    )(w_first.transpose(0, 2, 1), w_second.transpose(0, 2, 1), w_down)
    pieces = [packed]
    for step in range(1, chans):
        ring = [(i, (i + step) % chans) for i in range(chans)]
        pieces.append(lax.ppermute(packed, "chan", ring))

    pairs = []
    for col in range(bricks * reps):
        for c in range(chans):
            src = col + 2 * (c * planes // 4) - 1
            if 0 <= src < bricks * reps:
                ends = [(j // reps * chans + c) * reps + j % reps for j in (src, col)]
                pairs.append(tuple(ends))
    outward = lax.dynamic_slice_in_dim(features, (1 - side) * 4, 4, 1).transpose(1, 2, 0, 3)
    halo = lax.ppermute(outward, ("bricks", "chan", "rep"), pairs)

    edge, near, mat1, mat2, down_mat, back_mat = pl.pallas_call(
        local_kernel,
        out_shape=(
            jax.ShapeDtypeStruct((4, slabs, ROWS, 128), BF16),
            jax.ShapeDtypeStruct((4, slabs, ROWS, 128), BF16),
            jax.ShapeDtypeStruct((3, 1024, 256), BF16),
            jax.ShapeDtypeStruct((3, 1024, 256), BF16),
            jax.ShapeDtypeStruct((512, 256), BF16),
            jax.ShapeDtypeStruct((128, 1024), BF16),
        ),
        in_specs=[smem] + [vmem] * (1 + chans),
        out_specs=(vmem,) * 6,
        scratch_shapes=[
            pltpu.VMEM((62, 64, 128), BF16),
            pltpu.VMEM((54, 64, 128), BF16),
            pltpu.VMEM((8, slabs, ROWS, 128), BF16),
            pltpu.VMEM((slabs, 8, ROWS, 256), BF16),
        ],
        compiler_params=pltpu.CompilerParams(vmem_limit_bytes=36 << 20),
        cost_estimate=pl.CostEstimate(flops=6 * 6 * 512 * 1024 * 512, bytes_accessed=8 << 20, transcendentals=0),
        name="first_local",
    )(footprint, features.transpose(1, 2, 0, 3), *pieces)
    parts = jax.ShapeDtypeStruct((chans, 19, 64 // chans // reps, 128), F32)
    keep, send = pl.pallas_call(
        main_kernel,
        out_shape=(parts, parts),
        in_specs=[smem] + [vmem] * 9,
        out_specs=(vmem, vmem),
        scratch_shapes=[
            pltpu.VMEM((4, slabs, ROWS, 128), BF16),
            pltpu.VMEM((slabs + 2, 8, ROWS, 256), BF16),
            pltpu.VMEM((slabs + 2, 8, ROWS, 128), BF16),
            pltpu.VMEM((8, ROWS, 256), BF16),
            pltpu.VMEM((128, 128), F32),
            pltpu.VMEM((2, 2, ROWS, 128), BF16),
            pltpu.VMEM((256, 256), BF16),
            pltpu.VMEM((384, 1024), BF16),
            pltpu.VMEM((3, 384, 256), F32),
            pltpu.VMEM((256, 512), F32),
            pltpu.VMEM((8, 128), F32),
        ],
        compiler_params=pltpu.CompilerParams(vmem_limit_bytes=40 << 20),
        cost_estimate=pl.CostEstimate(flops=4 * 6 * 6 * 512 * 1024 * 512, bytes_accessed=16 << 20, transcendentals=0),
        name="head_and_grads",
    )(footprint, edge, halo, near, mat1, mat2, down_mat, back_mat, w_head.reshape(1, 64), labels[0])

    swap = [(i, 1 - i) for i in range(reps)]
    got = lax.ppermute(send, "rep", swap)
    mine = keep[0] + got[0]
    for step in range(1, chans):
        ring = [(i, (i + step) % chans) for i in range(chans)]
        mine = mine + lax.ppermute(keep[step] + got[step], "chan", ring)
    step = 1
    while step < bricks:
        mine = mine + lax.ppermute(mine, "bricks", [(i, i ^ step) for i in range(bricks)])
        step *= 2
    peer = lax.ppermute(mine, "rep", swap)
    share = 64 // chans
    second, down, head, loss = pl.pallas_call(
        final_kernel,
        out_shape=(
            jax.ShapeDtypeStruct((27, share, 64), F32),
            jax.ShapeDtypeStruct((8, share, 64), F32),
            jax.ShapeDtypeStruct((1, 64), F32),
            jax.ShapeDtypeStruct((1, 1), F32),
        ),
        in_specs=[smem, vmem, vmem],
        out_specs=(vmem,) * 4,
        name="assemble",
    )(footprint, mine, peer)
    return second.transpose(0, 2, 1), down, head.reshape(64), loss.reshape(1)


def solution(mesh):
    return jax.shard_map(
        shards,
        mesh=mesh,
        in_specs=(
            P(("groups", "bricks", "rep"), None, None, None, None),
            P(None, None, "chan"),
            P(None, None, "chan"),
            P(None, "chan", None),
            P(),
            P(None, "groups"),
            P(("groups", "bricks", "rep"), None, None),
        ),
        out_specs=(P("groups", None, "chan"), P("groups", "chan", None), P("groups"), P("groups")),
        check_vma=False,
    )
```

time: 149 us -> 86.2 us (0.58); the launches traced: 148 us -> 86.5 us
  local copies, waits for them, and re-layouts: 60.3 us -> 6.9 us
  Pallas kernels: 20.9 us -> 46.2 us
  starting transfers between devices: 34.8 us -> 10.8 us
  other arithmetic: 11 us -> 0.09 us
  waiting for transfers between devices: 17.4 us -> 21.7 us
  between operations: 3.39 us -> 0.75 us
    ppermute x7 -> x6, starting transfers between devices: 32.1 us -> 8.34 us  [the longest x2 3.96 us: shards(): lax.ppermute(mine, 'bricks', [(i, i ^ step) for i in range(bricks)])]
    reshape x10 -> x0, local copies, waits for them, and re-layouts: 22.6 us -> none  [the longest x4 16.6 us: arrange(): split.transpose(1, 2, 4, 5, 3, 0)]
    pallas_call x1 -> x3, Pallas kernels: 17.1 us -> 35.5 us  [the longest x1 31.7 us: shards(): pl.pallas_call(main_kernel, out_shape=(parts, parts), in_specs=[smem] + [...]
    another operation x3 -> x0, local copies, waits for them, and re-layouts: 8.77 us -> none  [the longest x1 5.42 us: arrange(): split = features.reshape(channels, width, rows // 4, 2, 2, depth)]
    pallas_call x1, Pallas kernels: 3.75 us -> 10.7 us  [shards(): pl.pallas_call(local_kernel, out_shape=(jax.ShapeDtypeStruct((4, slabs, R...]
    gather x4 -> x0, local copies, waits for them, and re-layouts: 6.66 us -> none  [gather_pieces(): return jnp.stack(pieces)[order]]
    concatenate x5 -> x0, other arithmetic: 5.71 us -> none  [the longest x1 1.98 us: gather_weights(): return jnp.concatenate([whole, whole], axis=2)]
    unnamed x22 -> x13, local copies, waits for them, and re-layouts: 9.52 us -> 4.59 us
  transfers between devices with their start and end apart: 8 -> 7, of which waited for: 5 -> 6; matrix products, arithmetic and copies ran while one was open for 34% -> 5% of each run, Pallas kernels for 3% -> 15%
where the time goes in v1:
time: 86.2 us; the launch traced here: 86.5 us
  Pallas kernels  46.2 us (54%)
  waiting for transfers between devices  21.7 us (25%)
  starting transfers between devices  10.8 us (13%)
  local copies, waits for them, and re-layouts  6.9 us (8%)
    pallas_call x1, Pallas kernels, shards(): pl.pallas_call(main_kernel, out_shape=(parts, parts), in_specs=[smem] + [...  31.7 us
    ppermute x2, waiting for transfers between devices, shards(): lax.ppermute(mine, 'bricks', [(i, i ^ step) for i in range(bricks)])  11.7 us
    pallas_call x1, Pallas kernels, shards(): pl.pallas_call(local_kernel, out_shape=(jax.ShapeDtypeStruct((4, slabs, R...  10.7 us
    unnamed x13, local copies, waits for them, and re-layouts  4.59 us
    ppermute x1, waiting for transfers between devices, shards(): mine = mine + lax.ppermute(keep[step] + got[step], 'chan', ring)  4.32 us
    ppermute x2, starting transfers between devices, shards(): lax.ppermute(mine, 'bricks', [(i, i ^ step) for i in range(bricks)])  3.96 us
    ppermute x1, waiting for transfers between devices, shards(): pieces.append(lax.ppermute(packed, 'chan', ring))  2.72 us
    ppermute x1, starting transfers between devices, shards(): mine = mine + lax.ppermute(keep[step] + got[step], 'chan', ring)  2.46 us
  transfers between devices with their start and end apart: 7, of which 6 were waited for; matrix products, arithmetic and copies ran while one was open for 5% of the time, Pallas kernels for 15%

profile of v1, /device:TPU:0, one launch (start us, length us, event | category | flops | bytes accessed | tf_op | source)
XLA Modules:
  0.0 86.5 jit_solution(14336315541036966807)
XLA Ops:
  0.6 1.7 %constant_dynamic-slice_fusion = bf16[1,64,4,24,128]{4,3,2,1,0:T(8,128)(2,1)S(1)} fusion(bf16[1,64,8,24,128]{4,3,2,1,0:T(8,128)(2,1)} %param.7, s32[]{:T(128)S(6)} %select_n.9), kind=kLoop, calls=%fused_computation.7 | loop fusion | bytes 3145732 | tf_op jit(solution)/shard_map/dynamic_slice | solution.py:387
  2.3 0.6 copy.16
  3.0 2.5 %collective-permute-start.1 = (bf16[4,24,64,128]{3,2,1,0:T(8,128)(2,1)S(1)}, bf16[4,24,64,128]{3,2,1,0:T(8,128)(2,1)S(1)}, u32[]{:S(2)}, u32[]{:S(2)}) collective-permute-start(bf16[4,24,64,128]{3,2,1,0:T(8,128)(2,1)S(1)} %bitcast.26), channel_id=1, source_target_pairs={{3,2},{0,1},{6,3},{1,4},{7,6},{4,5},{10,7},{5,8},{11,10},{8,9},{14... | collective-permute-start | bytes 4718600 | tf_op jit(solution)/shard_map/ppermute | solution.py:388
  5.4 1.9 %pack.1.refs_0_ = bf16[62,16,128]{2,1,0:T(8,128)(2,1)} custom-call(bf16[27,32,64]{2,1,0:T(8,128)(2,1)} %bitcast.27, bf16[27,32,64]{2,1,0:T(8,128)(2,1)} %bitcast.28, bf16[8,32,64]{2,1,0:T(8,128)(2,1)} %wd_ref.1), custom_call_target="tpu_custom_call" | custom-call | tf_op jit(solution)/shard_map/pack/pallas_call | solution.py:368
  7.3 0.0 copy-start
  7.3 0.0 copy-start.1
  7.3 1.8 %collective-permute-start = (bf16[62,16,128]{2,1,0:T(8,128)(2,1)}, bf16[62,16,128]{2,1,0:T(8,128)(2,1)S(1)}, u32[]{:S(2)}, u32[]{:S(2)}) collective-permute-start(bf16[62,16,128]{2,1,0:T(8,128)(2,1)} %pack.1.refs_0_), channel_id=1, source_target_pairs={{0,2},{2,0},{1,3},{3,1},{4,6},{6,4},{5,7},{7,5},{8,10},{10,8},{9,1... | collective-permute-start | bytes 761864 | tf_op jit(solution)/shard_map/ppermute | solution.py:378
  9.1 3.9 %copy.15 = bf16[1,64,8,24,128]{4,1,3,2,0:T(8,128)(2,1)S(1)} copy(bf16[1,64,8,24,128]{4,3,2,1,0:T(8,128)(2,1)} %param.7) | data formatting | bytes 6291456 | tf_op args[0]
  13.0 2.7 %collective-permute-done.refs_1_ = bf16[62,16,128]{2,1,0:T(8,128)(2,1)S(1)} collective-permute-done((bf16[62,16,128]{2,1,0:T(8,128)(2,1)}, bf16[62,16,128]{2,1,0:T(8,128)(2,1)S(1)}, u32[]{:S(2)}, u32[]{:S(2)}) %collective-permute-start) | collective-permute-done | bytes 253984 | tf_op jit(solution)/shard_map/ppermute | solution.py:378
  15.7 0.0 copy-done
  15.7 0.0 copy-done.1
  15.7 0.0 copy-start.2
  15.7 0.0 copy-start.3
  15.7 10.7 %first_local.1 = (bf16[4,6,256,128]{3,2,1,0:T(8,128)(2,1)S(1)}, bf16[4,6,256,128]{3,2,1,0:T(8,128)(2,1)S(1)}, bf16[3,1024,256]{2,1,0:T(8,128)(2,1)S(1)}, bf16[3,...) custom-call(s32[2,8]{1,0:T(2,128)S(1)} %copy-done.1, ...), custom_call_target="tpu_custom_call" | custom-call | flops 9663676416 | bytes 8388608 | tf_op jit(solution)/shard_map/first_local/pallas_call | solution.py:390
  26.5 0.0 collective-permute-done.1.halo_ref
  26.5 0.0 copy-done.2
  26.5 0.0 copy-done.3
  26.5 31.7 %head_and_grads.1 = (f32[2,19,16,128]{3,2,1,0:T(8,128)S(1)}, f32[2,19,16,128]{3,2,1,0:T(8,128)S(1)}) custom-call(s32[2,8]{1,0:T(2,128)S(1)} %copy-done.1, bf16[4,6,256,128]{3,2,1,0:T(8,128)(2,1)S(1)} %get-tuple-element.16.edge_ref, bf16[4,24,64,128]{3,2,1,0:T(8,128)(2,1)S(1)} %collective-permute-done.1.halo_ref, ...), custom_call_target="tpu_custom_call" | custom-call | flops 38654705664 | bytes 16777216 | tf_op jit(solution)/shard_map/head_and_grads/pallas_call | solution.py:413
  58.1 0.1 collective-permute-start.2
  58.2 1.6 %collective-permute-done.2 = f32[2,19,16,128]{3,2,1,0:T(8,128)S(1)} collective-permute-done((f32[2,19,16,128]{3,2,1,0:T(8,128)S(1)}, f32[2,19,16,128]{3,2,1,0:T(8,128)S(1)}, u32[]{:S(2)}, u32[]{:S(2)}) %collective-permute-start.2) | collective-permute-done | bytes 311328 | tf_op jit(solution)/shard_map/ppermute | solution.py:437
  59.8 2.5 %collective-permute-start.3 = (f32[19,16,128]{2,1,0:T(8,128)S(1)}, f32[19,16,128]{2,1,0:T(8,128)S(1)}, u32[]{:S(2)}, u32[]{:S(2)}) collective-permute-start(f32[19,16,128]{2,1,0:T(8,128)S(1)} %fusion), channel_id=1, source_target_pairs={{0,2},{2,0},{1,3},{3,1},{4,6},{6,4},{5,7},{7,5},{8,10},{10,8},{9,1... | collective-permute-start | bytes 466952 | tf_op jit(solution)/shard_map/ppermute | solution.py:441
  62.3 4.3 %collective-permute-done.3 = f32[19,16,128]{2,1,0:T(8,128)S(1)} collective-permute-done((f32[19,16,128]{2,1,0:T(8,128)S(1)}, f32[19,16,128]{2,1,0:T(8,128)S(1)}, u32[]{:S(2)}, u32[]{:S(2)}) %collective-permute-start.3) | collective-permute-done | bytes 155680 | tf_op jit(solution)/shard_map/ppermute | solution.py:441
  66.7 0.1 collective-permute-start.4
  66.7 5.5 %collective-permute-done.4 = f32[19,16,128]{2,1,0:T(8,128)S(1)} collective-permute-done((f32[19,16,128]{2,1,0:T(8,128)S(1)}, f32[19,16,128]{2,1,0:T(8,128)S(1)}, u32[]{:S(2)}, u32[]{:S(2)}) %collective-permute-start.4) | collective-permute-done | bytes 155680 | tf_op jit(solution)/shard_map/ppermute | solution.py:444
  72.3 3.9 %collective-permute-start.5 = (f32[19,16,128]{2,1,0:T(8,128)S(1)}, f32[19,16,128]{2,1,0:T(8,128)S(1)}, u32[]{:S(2)}, u32[]{:S(2)}) collective-permute-start(f32[19,16,128]{2,1,0:T(8,128)S(1)} %add.31), channel_id=1, source_target_pairs={{0,8},{4,12},{8,0},{12,4},{1,9},{5,13},{9,1},{13,5},{2,10},{6,14},... | collective-permute-start | bytes 466952 | tf_op jit(solution)/shard_map/ppermute | solution.py:444
  76.2 6.2 %collective-permute-done.5 = f32[19,16,128]{2,1,0:T(8,128)S(1)} collective-permute-done((f32[19,16,128]{2,1,0:T(8,128)S(1)}, f32[19,16,128]{2,1,0:T(8,128)S(1)}, u32[]{:S(2)}, u32[]{:S(2)}) %collective-permute-start.5) | collective-permute-done | bytes 155680 | tf_op jit(solution)/shard_map/ppermute | solution.py:444
  82.4 0.0 copy-start.4
  82.4 0.1 collective-permute-start.6
  82.5 1.4 %collective-permute-done.6.peer_ref = f32[19,16,128]{2,1,0:T(8,128)S(1)} collective-permute-done((f32[19,16,128]{2,1,0:T(8,128)S(1)}, f32[19,16,128]{2,1,0:T(8,128)S(1)}, u32[]{:S(2)}, u32[]{:S(2)}) %collective-permute-start.6) | collective-permute-done | bytes 155680 | tf_op jit(solution)/shard_map/ppermute | solution.py:446
  83.9 0.0 copy-done.4
  83.9 0.0 copy-start.5
  83.9 0.7 copy-done.5
  84.5 1.9 %assemble.1 = (f32[27,32,64]{2,1,0:T(8,128)}, f32[8,32,64]{2,1,0:T(8,128)}, f32[1,64]{1,0:T(1,128)}, f32[1,1]{1,0:T(1,128)}) custom-call(s32[2,8]{1,0:T(2,128)} %foot_ref.5, f32[19,16,128]{2,1,0:T(8,128)} %copy-done.4, f32[19,16,128]{2,1,0:T(8,128)} %copy-done.5), custom_call_target="tpu_custom_call" | custom-call | tf_op jit(solution)/shard_map/assemble/pallas_call | solution.py:448
  (4 shorter events, 0.1 us)
Async XLA Ops:
  3.0 23.5 %collective-permute-start.1 = (bf16[4,24,64,128]{3,2,1,0:T(8,128)(2,1)S(1)}, bf16[4,24,64,128]{3,2,1,0:T(8,128)(2,1)S(1)}, u32[]{:S(2)}, u32[]{:S(2)}) collective-permute-start(bf16[4,24,64,128]{3,2,1,0:T(8,128)(2,1)S(1)} %bitcast.26), channel_id=1, source_target_pairs={{3,2},{0,1},{6,3},{1,4},{7,6},{4,5},{10,7},{5,8},{11,10},{8,9},{14... | collective-permute-start | bytes 4718600 | tf_op jit(solution)/shard_map/ppermute | solution.py:388
  7.3 8.4 %copy-start = (bf16[62,16,128]{2,1,0:T(8,128)(2,1)S(1)}, bf16[62,16,128]{2,1,0:T(8,128)(2,1)}, u32[]{:S(2)}) copy-start(bf16[62,16,128]{2,1,0:T(8,128)(2,1)} %pack.1.refs_0_) | copy-start | bytes 761860
  7.3 8.4 %copy-start.1 = (s32[2,8]{1,0:T(2,128)S(1)}, s32[2,8]{1,0:T(2,128)}, u32[]{:S(2)}) copy-start(s32[2,8]{1,0:T(2,128)} %foot_ref.5) | copy-start | bytes 196
  7.3 8.4 %collective-permute-start = (bf16[62,16,128]{2,1,0:T(8,128)(2,1)}, bf16[62,16,128]{2,1,0:T(8,128)(2,1)S(1)}, u32[]{:S(2)}, u32[]{:S(2)}) collective-permute-start(bf16[62,16,128]{2,1,0:T(8,128)(2,1)} %pack.1.refs_0_), channel_id=1, source_target_pairs={{0,2},{2,0},{1,3},{3,1},{4,6},{6,4},{5,7},{7,5},{8,10},{10,8},{9,1... | collective-permute-start | bytes 761864 | tf_op jit(solution)/shard_map/ppermute | solution.py:378
  15.7 10.7 %copy-start.2 = (s32[1,4,768]{2,1,0:T(4,128)S(1)}, s32[1,4,768]{2,1,0:T(4,128)}, u32[]{:S(2)}) copy-start(s32[1,4,768]{2,1,0:T(4,128)} %param.13) | copy-start | bytes 36868
  15.7 10.7 %copy-start.3 = (f32[64]{0:T(128)S(1)}, f32[64]{0:T(128)}, u32[]{:S(2)}) copy-start(f32[64]{0:T(128)} %param.11) | copy-start | bytes 772
  58.1 1.7 %collective-permute-start.2 = (f32[2,19,16,128]{3,2,1,0:T(8,128)S(1)}, f32[2,19,16,128]{3,2,1,0:T(8,128)S(1)}, u32[]{:S(2)}, u32[]{:S(2)}) collective-permute-start(f32[2,19,16,128]{3,2,1,0:T(8,128)S(1)} %get-tuple-element.23), channel_id=1, source_target_pairs={{0,1},{1,0},{2,3},{3,2},{4,5},{5,4},{6,7},{7,6},{8,9},{9,8},{10,11... | collective-permute-start | bytes 933896 | tf_op jit(solution)/shard_map/ppermute | solution.py:437
  59.8 6.8 %collective-permute-start.3 = (f32[19,16,128]{2,1,0:T(8,128)S(1)}, f32[19,16,128]{2,1,0:T(8,128)S(1)}, u32[]{:S(2)}, u32[]{:S(2)}) collective-permute-start(f32[19,16,128]{2,1,0:T(8,128)S(1)} %fusion), channel_id=1, source_target_pairs={{0,2},{2,0},{1,3},{3,1},{4,6},{6,4},{5,7},{7,5},{8,10},{10,8},{9,1... | collective-permute-start | bytes 466952 | tf_op jit(solution)/shard_map/ppermute | solution.py:441
  66.7 5.6 %collective-permute-start.4 = (f32[19,16,128]{2,1,0:T(8,128)S(1)}, f32[19,16,128]{2,1,0:T(8,128)S(1)}, u32[]{:S(2)}, u32[]{:S(2)}) collective-permute-start(f32[19,16,128]{2,1,0:T(8,128)S(1)} %fusion.2), channel_id=1, source_target_pairs={{0,4},{4,0},{8,12},{12,8},{1,5},{5,1},{9,13},{13,9},{2,6},{6,2},{1... | collective-permute-start | bytes 466952 | tf_op jit(solution)/shard_map/ppermute | solution.py:444
  72.3 10.1 %collective-permute-start.5 = (f32[19,16,128]{2,1,0:T(8,128)S(1)}, f32[19,16,128]{2,1,0:T(8,128)S(1)}, u32[]{:S(2)}, u32[]{:S(2)}) collective-permute-start(f32[19,16,128]{2,1,0:T(8,128)S(1)} %add.31), channel_id=1, source_target_pairs={{0,8},{4,12},{8,0},{12,4},{1,9},{5,13},{9,1},{13,5},{2,10},{6,14},... | collective-permute-start | bytes 466952 | tf_op jit(solution)/shard_map/ppermute | solution.py:444
  82.4 1.5 %copy-start.4 = (f32[19,16,128]{2,1,0:T(8,128)}, f32[19,16,128]{2,1,0:T(8,128)S(1)}, u32[]{:S(2)}) copy-start(f32[19,16,128]{2,1,0:T(8,128)S(1)} %add.32.mine_ref) | copy-start | bytes 466948
  82.4 1.4 %collective-permute-start.6 = (f32[19,16,128]{2,1,0:T(8,128)S(1)}, f32[19,16,128]{2,1,0:T(8,128)S(1)}, u32[]{:S(2)}, u32[]{:S(2)}) collective-permute-start(f32[19,16,128]{2,1,0:T(8,128)S(1)} %add.32.mine_ref), channel_id=1, source_target_pairs={{0,1},{1,0},{2,3},{3,2},{4,5},{5,4},{6,7},{7,6},{8,9},{9,8},{10,11... | collective-permute-start | bytes 466952 | tf_op jit(solution)/shard_map/ppermute | solution.py:446
  83.9 0.7 copy-start.5

commit v2 on v1

--- a/solution.py
+++ b/solution.py
@@ -42,8 +42,10 @@
                     out_ref[e, row : row + 64, rx * 128 : rx * 128 + 128] = merge_half(*halves)
 
 
-def conv_block(window_ref, slot, par, w_ref):
-    lhs = jnp.concatenate([window_ref[slot, 2 * k + par] for k in range(4)], axis=1)
+def conv_rows(window_ref, w_ref, slot=()):
+    lhs = jnp.concatenate(
+        [window_ref[(*slot, pl.ds(2 * k, 2))].reshape(2 * ROWS, 256) for k in range(4)], axis=1
+    )
     below, level, above = [jnp.dot(lhs, w_ref[e], preferred_element_type=F32) for e in range(3)]
     return level + shifted(below, 2) + shifted(above, -2)
 
@@ -60,9 +62,9 @@
         dst_ref[plane, t, 128 * py : 128 * py + 128] = tall.T
 
 
-def fill_window(window_ref, slot, plane, src_ref, src_plane, index, count):
-    window_ref[slot, plane, :, 0:128] = gated(src_ref, src_plane, index, count)
-    window_ref[slot, plane, :, 128:256] = merge_half(
+def fill_window(window_ref, plane, src_ref, src_plane, index, count):
+    window_ref[plane, :, 0:128] = gated(src_ref, src_plane, index, count)
+    window_ref[plane, :, 128:256] = merge_half(
         gated(src_ref, src_plane, index + 1, count), gated(src_ref, src_plane, index - 1, count)
     )
 
@@ -79,7 +81,8 @@
 def local_kernel(foot_ref, feat_ref, *refs):
     chans = lax.axis_size("chan")
     piece_refs = refs[:chans]
-    edge_ref, y1_ref, m1_ref, m2_ref, down_ref, back_ref, whole, turned, arranged, window = refs[chans:]
+    edge_ref, y1_ref, m1_ref, m2_ref, down_ref, back_ref, whole, turned, arranged = refs[chans:-2]
+    even_window, odd_window = refs[-2:]
     column = lax.axis_index("bricks") * lax.axis_size("rep") + lax.axis_index("rep")
     me = lax.axis_index("chan")
     side = me * (BRICK // chans) // 4
@@ -115,21 +118,25 @@
 
     lax.fori_loop(0, count, turn, 0)
 
-    def fill(t, carry):
+    def fill(window, t):
         for p in range(8):
-            fill_window(window, t, p, arranged, p, t, count)
+            fill_window(window, p, arranged, p, t, count)
+
+    def conv(window, t):
+        out = jnp.maximum(conv_rows(window, m1_ref), 0.0).astype(BF16)
+        for par in range(2):
+            for rx in range(2):
+                y1_ref[2 * rx + par, t] = out[ROWS * par : ROWS * par + ROWS, 128 * rx : 128 * rx + 128]
+
+    def pair(j, carry):
+        fill(odd_window, 2 * j + 1)
+        conv(even_window, 2 * j)
+        fill(even_window, 2 * j + 2)
+        conv(odd_window, 2 * j + 1)
         return carry
 
-    lax.fori_loop(0, count, fill, 0)
-
-    def conv(t, carry):
-        for par in range(2):
-            out = jnp.maximum(conv_block(window, t, par, m1_ref), 0.0).astype(BF16)
-            for rx in range(2):
-                y1_ref[2 * rx + par, t] = out[:, 128 * rx : 128 * rx + 128]
-        return carry
-
-    lax.fori_loop(0, count, conv, 0)
+    fill(even_window, 0)
+    lax.fori_loop(0, count // 2, pair, 0)
 
 
 def main_kernel(
@@ -146,7 +153,8 @@
     keep_ref,
     send_ref,
     arranged,
-    window,
+    even_window,
+    odd_window,
     hidden,
     hwin,
     headm_ref,
@@ -177,7 +185,11 @@
     square_row = lax.broadcasted_iota(jnp.int32, (128, 128), 0)
     square_lane = lax.broadcasted_iota(jnp.int32, (128, 128), 1)
     same_half = (square_row < 64) == (square_lane < 64)
-    headm_ref[...] = jnp.where(same_half, jnp.broadcast_to(head_row, (128, 128)).T, 0.0)
+    head_mat = jnp.where(same_half, jnp.broadcast_to(head_row, (128, 128)).T, 0.0)
+    head_high = head_mat.astype(BF16)
+    headm_ref[0:128] = head_high
+    headm_ref[128:256] = head_high
+    headm_ref[256:384] = (head_mat - head_high.astype(F32)).astype(BF16)
     pick_depth = jnp.where(square_row // 2 == square_lane % 64, 1.0, 0.0).astype(BF16)
 
     def turn(t, carry):
@@ -187,107 +199,129 @@
 
     lax.fori_loop(0, other_count, turn, 0)
 
-    def fill(slot, carry):
-        t = slot - 1
+    def fill(window, t):
         for p in range(4):
-            fill_window(window, slot, (1 - side) * 4 + p, edge_ref, p, t, count)
-            fill_window(window, slot, side * 4 + p, arranged, p, t - offset, other_count)
-        return carry
-
-    lax.fori_loop(0, count + 2, fill, 0)
-
-    def first(slot, carry):
-        t = slot - 1
+            fill_window(window, (1 - side) * 4 + p, edge_ref, p, t, count)
+            fill_window(window, side * 4 + p, arranged, p, t - offset, other_count)
+
+    def first(window, t):
         own = (t >= 0) & (t < count)
         next_to = (t - offset >= 0) & (t - offset < other_count)
-        for par in range(2):
-            out = jnp.maximum(conv_block(window, slot, par, m1_ref), 0.0).astype(BF16)
-            for rx in range(2):
-                live = jnp.where(side == rx, next_to, own)
-                block = out[:, 128 * rx : 128 * rx + 128]
-                hidden[slot, side * 4 + 2 * rx + par] = jnp.where(
-                    live, block, jnp.zeros_like(block)
-                )
+        out = jnp.maximum(conv_rows(window, m1_ref), 0.0).astype(BF16)
+        for rx in range(2):
+            live = jnp.where(side == rx, next_to, own)
+            for par in range(2):
+                block = out[ROWS * par : ROWS * par + ROWS, 128 * rx : 128 * rx + 128]
+                hidden[t + 1, side * 4 + 2 * rx + par] = jnp.where(live, block, jnp.zeros_like(block))
+
+    def near(t):
         for p in range(4):
-            hidden[slot, (1 - side) * 4 + p] = gated(near_ref, p, t, count)
+            hidden[t + 1, (1 - side) * 4 + p] = gated(near_ref, p, t, count)
+
+    def rim(i, carry):
+        t = jnp.where(i == 0, -1, count)
+        beside = (t - offset >= 0) & (t - offset < other_count)
+        hidden[t + 1] = jnp.zeros((8, ROWS, 128), BF16)
+
+        @pl.when(beside)
+        def _():
+            fill(even_window, t)
+            first(even_window, t)
+
         return carry
 
-    lax.fori_loop(0, count + 2, first, 0)
-
-    even = square_row % 2 == 0
-
-    def second(t, carry):
-        for p in range(8):
-            hwin[p, :, 0:128] = hidden[t + 1, p]
-            hwin[p, :, 128:256] = merge_half(hidden[t + 2, p], hidden[t, p])
-        for par in range(2):
-            lhs = jnp.concatenate([hwin[2 * k + par] for k in range(4)], axis=1)
-            below, level, above = [
-                jnp.dot(lhs, m2_ref[e], preferred_element_type=F32) for e in range(3)
-            ]
-            out = level + shifted(below, 2) + shifted(above, -2)
-            out = jnp.maximum(out, 0.0).astype(BF16)
-            for rx in range(2):
-                y2_ref[rx, par] = out[:, 128 * rx : 128 * rx + 128]
-        for rx in range(2):
-            fine = jnp.concatenate(
-                [y2_ref[rx, a, 128 * b : 128 * b + 128] for a in range(2) for b in range(2)], axis=1
-            )
-            both = jnp.dot(fine, down_mat[...], preferred_element_type=F32)
-            coarse = both[:, 0:128] + shifted(both[:, 128:256], -1)
-            rect = jnp.maximum(coarse, 0.0)
-            logit = jnp.dot(
-                rect, headm_ref[...], precision=lax.Precision.HIGHEST, preferred_element_type=F32
-            )
-            plane = 4 * side + 2 * rx
-            keep = even & (plane >= mine) & (plane < mine + planes)
-            line = label_ref[:, pl.ds(pl.multiple_of(128 * t, 128), 128)].astype(F32)
-            row = jnp.where(side == 1, line[2 + rx : 3 + rx], line[rx : rx + 1])
-            row = jnp.broadcast_to(row, (128, 128))
-            row = jnp.where(same_half, row, 0.0).astype(BF16)
-            label = lax.dot_general(
-                pick_depth, row, (((1,), (1,)), ((), ())), preferred_element_type=F32
-            )
-            tail = jnp.exp(-jnp.abs(logit))
-            soft = jnp.maximum(logit, 0.0) + jnp.log1p(tail)
-            sigmoid = jnp.where(logit >= 0.0, 1.0, tail) / (1.0 + tail)
-            loss = jnp.where(keep, soft - label * logit, 0.0)
-            slope = jnp.where(keep, (sigmoid - label) * (1.0 / COARSE), 0.0)
-            small[0:1] += jnp.sum(slope * rect, axis=0, keepdims=True)
-            small[1:2] += jnp.sum(loss, axis=0, keepdims=True)
-            delta = jnp.where(coarse > 0.0, slope * head_row, 0.0).astype(BF16).astype(F32)
-            moved = shifted(delta, 1)
-            delta_t[0:128, 128 * rx : 128 * rx + 128] = delta.T.astype(BF16)
-            delta_t[128:256, 128 * rx : 128 * rx + 128] = moved.T.astype(BF16)
-            spread = (delta + moved).astype(BF16)
-            back = jnp.dot(spread, back_mat[...], preferred_element_type=F32)
-            for a in range(2):
-                for b in range(2):
-                    lane = (2 * a + b) * 256
-                    err = jnp.where(even, back[:, lane : lane + 128], back[:, lane + 128 : lane + 256])
-                    live = y2_ref[rx, a, 128 * b : 128 * b + 128].astype(F32) > 0.0
-                    err = jnp.where(live, err, 0.0)
-                    col = (2 * rx + a) * 256 + b * 128
-                    turned = err.astype(BF16).T.astype(F32)
-                    up = jnp.where(square_lane < 126, pltpu.roll(turned, 126, 1), 0.0)
-                    down = jnp.where(square_lane >= 2, pltpu.roll(turned, 2, 1), 0.0)
-                    for e, value in enumerate((up, turned, down)):
-                        err_t[128 * e : 128 * e + 128, col : col + 128] = value.astype(BF16)
+    def pair(j, carry):
+        fill(odd_window, 2 * j + 1)
+        near(2 * j)
+        first(even_window, 2 * j)
+        fill(even_window, 2 * j + 2)
+        near(2 * j + 1)
+        first(odd_window, 2 * j + 1)
+        return carry
+
+    lax.fori_loop(0, 2, rim, 0)
+    fill(even_window, 0)
+    lax.fori_loop(0, count // 2, pair, 0)
+
+    row4 = lax.broadcasted_iota(jnp.int32, (512, 128), 0)
+    even4 = row4 % 2 == 0
+    plane4 = 4 * side + 2 * (row4 // 128 % 2)
+    keep = even4 & (plane4 >= mine) & (plane4 < mine + planes)
+
+    def second(j, carry):
+        for u in range(2):
+            t = 2 * j + u
+            for p in range(8):
+                hwin[u, p, :, 0:128] = hidden[t + 1, p]
+                hwin[u, p, :, 128:256] = merge_half(hidden[t + 2, p], hidden[t, p])
+            out = jnp.maximum(conv_rows(hwin, m2_ref, (u,)), 0.0).astype(BF16)
+            for par in range(2):
+                for rx in range(2):
+                    y2_ref[u, rx, par] = out[ROWS * par : ROWS * par + ROWS, 128 * rx : 128 * rx + 128]
         fine = jnp.concatenate(
             [
-                jnp.concatenate([y2_ref[rx, a, 128 * b : 128 * b + 128] for rx in range(2)], axis=0)
+                jnp.concatenate(
+                    [y2_ref[u, rx, a, 128 * b : 128 * b + 128] for u in range(2) for rx in range(2)],
+                    axis=0,
+                )
                 for a in range(2)
                 for b in range(2)
             ],
             axis=1,
         )
+        both = jnp.dot(fine, down_mat[...], preferred_element_type=F32)
+        coarse = both[:, 0:128] + shifted(both[:, 128:256], -1)
+        rect = jnp.maximum(coarse, 0.0)
+        high = rect.astype(BF16)
+        rest = (rect - high.astype(F32)).astype(BF16)
+        logit = jnp.dot(
+            jnp.concatenate([high, rest, high], axis=1), headm_ref[...], preferred_element_type=F32
+        )
+        labels = []
+        for u in range(2):
+            line = label_ref[:, pl.ds(pl.multiple_of(256 * j + 128 * u, 128), 128)].astype(F32)
+            for rx in range(2):
+                row = jnp.where(side == 1, line[2 + rx : 3 + rx], line[rx : rx + 1])
+                row = jnp.where(same_half, jnp.broadcast_to(row, (128, 128)), 0.0).astype(BF16)
+                labels.append(
+                    lax.dot_general(
+                        pick_depth, row, (((1,), (1,)), ((), ())), preferred_element_type=F32
+                    )
+                )
+        label = jnp.concatenate(labels, axis=0)
+        tail = jnp.exp(-jnp.abs(logit))
+        soft = jnp.maximum(logit, 0.0) + jnp.log1p(tail)
+        sigmoid = jnp.where(logit >= 0.0, 1.0, tail) / (1.0 + tail)
+        loss = jnp.where(keep, soft - label * logit, 0.0)
+        slope = jnp.where(keep, (sigmoid - label) * (1.0 / COARSE), 0.0)
+        small[0:1] += jnp.sum(slope * rect, axis=0, keepdims=True)
+        small[1:2] += jnp.sum(loss, axis=0, keepdims=True)
+        delta = jnp.where(coarse > 0.0, slope * head_row, 0.0).astype(BF16).astype(F32)
+        moved = shifted(delta, 1)
+        delta_t[0:128] = delta.astype(BF16).T
+        delta_t[128:256] = moved.astype(BF16).T
+        back = jnp.dot((delta + moved).astype(BF16), back_mat[...], preferred_element_type=F32)
+        for a in range(2):
+            for b in range(2):
+                lane = (2 * a + b) * 256
+                err = jnp.where(even4, back[:, lane : lane + 128], back[:, lane + 128 : lane + 256])
+                live = fine[:, lane // 2 : lane // 2 + 128].astype(F32) > 0.0
+                err = jnp.where(live, err, 0.0)
+                for n in range(4):
+                    turned = err[128 * n : 128 * n + 128].astype(BF16).T
+                    col = n * 512 + a * 256 + b * 128
+                    err_t[128:256, col : col + 128] = turned
+                    up = jnp.where(square_lane < 126, pltpu.roll(turned, 126, 1), jnp.zeros_like(turned))
+                    down = jnp.where(square_lane >= 2, pltpu.roll(turned, 2, 1), jnp.zeros_like(turned))
+                    err_t[0:128, col : col + 128] = up
+                    err_t[256:384, col : col + 128] = down
         grad_down[...] += jnp.dot(delta_t[...], fine, preferred_element_type=F32)
         for a in range(3):
-            rows = hwin[2 * a : 2 * a + 4].reshape(4 * ROWS, 256)
+            rows = hwin[:, 2 * a : 2 * a + 4].reshape(8 * ROWS, 256)
             grad[a] += jnp.dot(err_t[...], rows, preferred_element_type=F32)
         return carry
 
-    lax.fori_loop(0, count, second, 0)
+    lax.fori_loop(0, count // 2, second, 0)
 
     low = lanes_low((64, 128))
     rep, chan = lax.axis_index("rep"), lax.axis_index("chan")
@@ -403,7 +437,8 @@
             pltpu.VMEM((62, 64, 128), BF16),
             pltpu.VMEM((54, 64, 128), BF16),
             pltpu.VMEM((8, slabs, ROWS, 128), BF16),
-            pltpu.VMEM((slabs, 8, ROWS, 256), BF16),
+            pltpu.VMEM((8, ROWS, 256), BF16),
+            pltpu.VMEM((8, ROWS, 256), BF16),
         ],
         compiler_params=pltpu.CompilerParams(vmem_limit_bytes=36 << 20),
         cost_estimate=pl.CostEstimate(flops=6 * 6 * 512 * 1024 * 512, bytes_accessed=8 << 20, transcendentals=0),
@@ -417,13 +452,14 @@
         out_specs=(vmem, vmem),
         scratch_shapes=[
             pltpu.VMEM((4, slabs, ROWS, 128), BF16),
-            pltpu.VMEM((slabs + 2, 8, ROWS, 256), BF16),
+            pltpu.VMEM((8, ROWS, 256), BF16),
+            pltpu.VMEM((8, ROWS, 256), BF16),
             pltpu.VMEM((slabs + 2, 8, ROWS, 128), BF16),
-            pltpu.VMEM((8, ROWS, 256), BF16),
-            pltpu.VMEM((128, 128), F32),
-            pltpu.VMEM((2, 2, ROWS, 128), BF16),
-            pltpu.VMEM((256, 256), BF16),
-            pltpu.VMEM((384, 1024), BF16),
+            pltpu.VMEM((2, 8, ROWS, 256), BF16),
+            pltpu.VMEM((384, 128), BF16),
+            pltpu.VMEM((2, 2, 2, ROWS, 128), BF16),
+            pltpu.VMEM((256, 512), BF16),
+            pltpu.VMEM((384, 2048), BF16),
             pltpu.VMEM((3, 384, 256), F32),
             pltpu.VMEM((256, 512), F32),
             pltpu.VMEM((8, 128), F32),

time: 86.2 us -> 79.8 us (0.926)
  Pallas kernels: 46.2 us -> 18.9 us
  starting transfers between devices: 10.8 us -> 31.9 us
    ppermute x1, starting transfers between devices: 0.07 us -> 21.1 us  [shards(): got = lax.ppermute(send, 'rep', swap)]
    pallas_call x1, Pallas kernels: 31.7 us -> 10.9 us  [shards(): pl.pallas_call(main_kernel, out_shape=(parts, parts), in_specs=[smem] + [...]
    pallas_call x1, Pallas kernels: 10.7 us -> 4.12 us  [shards(): pl.pallas_call(local_kernel, out_shape=(jax.ShapeDtypeStruct((4, slabs, R...]
    ppermute x1, starting transfers between devices: 2.46 us -> 4.09 us  [shards(): mine = mine + lax.ppermute(keep[step] + got[step], 'chan', ring)]
    ppermute x2, starting transfers between devices: 3.96 us -> 2.47 us  [shards(): lax.ppermute(mine, 'bricks', [(i, i ^ step) for i in range(bricks)])]
  transfers between devices with their start and end apart: 7 -> 7, of which waited for: 6 -> 6; matrix products, arithmetic and copies ran while one was open for 5% -> 5% of each run, Pallas kernels for 15% -> 7%
where the time goes in v2:
time: 79.8 us; the launch traced here: 80.8 us
  starting transfers between devices  31.9 us (40%)
  waiting for transfers between devices  22.3 us (28%)
  Pallas kernels  18.9 us (24%)
  local copies, waits for them, and re-layouts  6.9 us (9%)
    ppermute x1, starting transfers between devices, shards(): got = lax.ppermute(send, 'rep', swap)  21.1 us
    ppermute x2, waiting for transfers between devices, shards(): lax.ppermute(mine, 'bricks', [(i, i ^ step) for i in range(bricks)])  12.5 us
    pallas_call x1, Pallas kernels, shards(): pl.pallas_call(main_kernel, out_shape=(parts, parts), in_specs=[smem] + [...  10.9 us
    unnamed x13, local copies, waits for them, and re-layouts  4.59 us
    ppermute x1, waiting for transfers between devices, shards(): mine = mine + lax.ppermute(keep[step] + got[step], 'chan', ring)  4.55 us
    pallas_call x1, Pallas kernels, shards(): pl.pallas_call(local_kernel, out_shape=(jax.ShapeDtypeStruct((4, slabs, R...  4.12 us
    ppermute x1, starting transfers between devices, shards(): mine = mine + lax.ppermute(keep[step] + got[step], 'chan', ring)  4.09 us
    ppermute x1, waiting for transfers between devices, shards(): pieces.append(lax.ppermute(packed, 'chan', ring))  2.72 us
  transfers between devices with their start and end apart: 7, of which 6 were waited for; matrix products, arithmetic and copies ran while one was open for 5% of the time, Pallas kernels for 7%

profile of v2, /device:TPU:0, one launch (start us, length us, event | category | flops | bytes accessed | tf_op | source)
XLA Modules:
  0.0 80.8 jit_solution(17067863215235123420)
XLA Ops:
  0.6 1.7 %constant_dynamic-slice_fusion = bf16[1,64,4,24,128]{4,3,2,1,0:T(8,128)(2,1)S(1)} fusion(bf16[1,64,8,24,128]{4,3,2,1,0:T(8,128)(2,1)} %param.7, s32[]{:T(128)S(6)} %select_n.9), kind=kLoop, calls=%fused_computation.7 | loop fusion | bytes 3145732 | tf_op jit(solution)/shard_map/dynamic_slice | solution.py:421
  2.3 0.6 copy.16
  3.0 2.5 %collective-permute-start.1 = (bf16[4,24,64,128]{3,2,1,0:T(8,128)(2,1)S(1)}, bf16[4,24,64,128]{3,2,1,0:T(8,128)(2,1)S(1)}, u32[]{:S(2)}, u32[]{:S(2)}) collective-permute-start(bf16[4,24,64,128]{3,2,1,0:T(8,128)(2,1)S(1)} %bitcast.26), channel_id=1, source_target_pairs={{3,2},{0,1},{6,3},{1,4},{7,6},{4,5},{10,7},{5,8},{11,10},{8,9},{14... | collective-permute-start | bytes 4718600 | tf_op jit(solution)/shard_map/ppermute | solution.py:422
  5.4 1.9 %pack.1.refs_0_ = bf16[62,16,128]{2,1,0:T(8,128)(2,1)} custom-call(bf16[27,32,64]{2,1,0:T(8,128)(2,1)} %bitcast.27, bf16[27,32,64]{2,1,0:T(8,128)(2,1)} %bitcast.28, bf16[8,32,64]{2,1,0:T(8,128)(2,1)} %wd_ref.1), custom_call_target="tpu_custom_call" | custom-call | tf_op jit(solution)/shard_map/pack/pallas_call | solution.py:402
  7.3 0.0 copy-start
  7.3 0.0 copy-start.1
  7.3 1.8 %collective-permute-start = (bf16[62,16,128]{2,1,0:T(8,128)(2,1)}, bf16[62,16,128]{2,1,0:T(8,128)(2,1)S(1)}, u32[]{:S(2)}, u32[]{:S(2)}) collective-permute-start(bf16[62,16,128]{2,1,0:T(8,128)(2,1)} %pack.1.refs_0_), channel_id=1, source_target_pairs={{0,2},{2,0},{1,3},{3,1},{4,6},{6,4},{5,7},{7,5},{8,10},{10,8},{9,1... | collective-permute-start | bytes 761864 | tf_op jit(solution)/shard_map/ppermute | solution.py:412
  9.1 3.9 %copy.15 = bf16[1,64,8,24,128]{4,1,3,2,0:T(8,128)(2,1)S(1)} copy(bf16[1,64,8,24,128]{4,3,2,1,0:T(8,128)(2,1)} %param.7) | data formatting | bytes 6291456 | tf_op args[0]
  13.0 2.7 %collective-permute-done.refs_1_ = bf16[62,16,128]{2,1,0:T(8,128)(2,1)S(1)} collective-permute-done((bf16[62,16,128]{2,1,0:T(8,128)(2,1)}, bf16[62,16,128]{2,1,0:T(8,128)(2,1)S(1)}, u32[]{:S(2)}, u32[]{:S(2)}) %collective-permute-start) | collective-permute-done | bytes 253984 | tf_op jit(solution)/shard_map/ppermute | solution.py:412
  15.7 0.0 copy-done
  15.7 0.0 copy-done.1
  15.7 0.0 copy-start.2
  15.7 0.0 copy-start.3
  15.7 4.1 %first_local.1 = (bf16[4,6,256,128]{3,2,1,0:T(8,128)(2,1)S(1)}, bf16[4,6,256,128]{3,2,1,0:T(8,128)(2,1)S(1)}, bf16[3,1024,256]{2,1,0:T(8,128)(2,1)S(1)}, bf16[3,...) custom-call(s32[2,8]{1,0:T(2,128)S(1)} %copy-done.1, ...), custom_call_target="tpu_custom_call" | custom-call | flops 9663676416 | bytes 8388608 | tf_op jit(solution)/shard_map/first_local/pallas_call | solution.py:424
  19.9 0.0 collective-permute-done.1.halo_ref
  19.9 0.0 copy-done.2
  19.9 0.0 copy-done.3
  19.9 10.9 %head_and_grads.1 = (f32[2,19,16,128]{3,2,1,0:T(8,128)S(1)}, f32[2,19,16,128]{3,2,1,0:T(8,128)S(1)}) custom-call(s32[2,8]{1,0:T(2,128)S(1)} %copy-done.1, bf16[4,6,256,128]{3,2,1,0:T(8,128)(2,1)S(1)} %get-tuple-element.16.edge_ref, bf16[4,24,64,128]{3,2,1,0:T(8,128)(2,1)S(1)} %collective-permute-done.1.halo_ref, ...), custom_call_target="tpu_custom_call" | custom-call | flops 38654705664 | bytes 16777216 | tf_op jit(solution)/shard_map/head_and_grads/pallas_call | solution.py:448
  30.8 21.1 %collective-permute-start.2 = (f32[2,19,16,128]{3,2,1,0:T(8,128)S(1)}, f32[2,19,16,128]{3,2,1,0:T(8,128)S(1)}, u32[]{:S(2)}, u32[]{:S(2)}) collective-permute-start(f32[2,19,16,128]{3,2,1,0:T(8,128)S(1)} %get-tuple-element.23), channel_id=1, source_target_pairs={{0,1},{1,0},{2,3},{3,2},{4,5},{5,4},{6,7},{7,6},{8,9},{9,8},{10,11... | collective-permute-start | bytes 933896 | tf_op jit(solution)/shard_map/ppermute | solution.py:473
  51.9 1.2 %collective-permute-done.2 = f32[2,19,16,128]{3,2,1,0:T(8,128)S(1)} collective-permute-done((f32[2,19,16,128]{3,2,1,0:T(8,128)S(1)}, f32[2,19,16,128]{3,2,1,0:T(8,128)S(1)}, u32[]{:S(2)}, u32[]{:S(2)}) %collective-permute-start.2) | collective-permute-done | bytes 311328 | tf_op jit(solution)/shard_map/ppermute | solution.py:473
  53.1 4.1 %collective-permute-start.3 = (f32[19,16,128]{2,1,0:T(8,128)S(1)}, f32[19,16,128]{2,1,0:T(8,128)S(1)}, u32[]{:S(2)}, u32[]{:S(2)}) collective-permute-start(f32[19,16,128]{2,1,0:T(8,128)S(1)} %fusion), channel_id=1, source_target_pairs={{0,2},{2,0},{1,3},{3,1},{4,6},{6,4},{5,7},{7,5},{8,10},{10,8},{9,1... | collective-permute-start | bytes 466952 | tf_op jit(solution)/shard_map/ppermute | solution.py:477
  57.2 4.5 %collective-permute-done.3 = f32[19,16,128]{2,1,0:T(8,128)S(1)} collective-permute-done((f32[19,16,128]{2,1,0:T(8,128)S(1)}, f32[19,16,128]{2,1,0:T(8,128)S(1)}, u32[]{:S(2)}, u32[]{:S(2)}) %collective-permute-start.3) | collective-permute-done | bytes 155680 | tf_op jit(solution)/shard_map/ppermute | solution.py:477
  61.8 2.1 %collective-permute-start.4 = (f32[19,16,128]{2,1,0:T(8,128)S(1)}, f32[19,16,128]{2,1,0:T(8,128)S(1)}, u32[]{:S(2)}, u32[]{:S(2)}) collective-permute-start(f32[19,16,128]{2,1,0:T(8,128)S(1)} %fusion.2), channel_id=1, source_target_pairs={{0,4},{4,0},{8,12},{12,8},{1,5},{5,1},{9,13},{13,9},{2,6},{6,2},{1... | collective-permute-start | bytes 466952 | tf_op jit(solution)/shard_map/ppermute | solution.py:480
  63.8 3.7 %collective-permute-done.4 = f32[19,16,128]{2,1,0:T(8,128)S(1)} collective-permute-done((f32[19,16,128]{2,1,0:T(8,128)S(1)}, f32[19,16,128]{2,1,0:T(8,128)S(1)}, u32[]{:S(2)}, u32[]{:S(2)}) %collective-permute-start.4) | collective-permute-done | bytes 155680 | tf_op jit(solution)/shard_map/ppermute | solution.py:480
  67.6 0.4 collective-permute-start.5
  68.0 8.7 %collective-permute-done.5 = f32[19,16,128]{2,1,0:T(8,128)S(1)} collective-permute-done((f32[19,16,128]{2,1,0:T(8,128)S(1)}, f32[19,16,128]{2,1,0:T(8,128)S(1)}, u32[]{:S(2)}, u32[]{:S(2)}) %collective-permute-start.5) | collective-permute-done | bytes 155680 | tf_op jit(solution)/shard_map/ppermute | solution.py:480
  76.8 0.0 copy-start.4
  76.8 0.1 collective-permute-start.6
  76.9 1.4 %collective-permute-done.6.peer_ref = f32[19,16,128]{2,1,0:T(8,128)S(1)} collective-permute-done((f32[19,16,128]{2,1,0:T(8,128)S(1)}, f32[19,16,128]{2,1,0:T(8,128)S(1)}, u32[]{:S(2)}, u32[]{:S(2)}) %collective-permute-start.6) | collective-permute-done | bytes 155680 | tf_op jit(solution)/shard_map/ppermute | solution.py:482
  78.2 0.0 copy-done.4
  78.2 0.0 copy-start.5
  78.2 0.7 copy-done.5
  78.9 1.9 %assemble.1 = (f32[27,32,64]{2,1,0:T(8,128)}, f32[8,32,64]{2,1,0:T(8,128)}, f32[1,64]{1,0:T(1,128)}, f32[1,1]{1,0:T(1,128)}) custom-call(s32[2,8]{1,0:T(2,128)} %foot_ref.5, f32[19,16,128]{2,1,0:T(8,128)} %copy-done.4, f32[19,16,128]{2,1,0:T(8,128)} %copy-done.5), custom_call_target="tpu_custom_call" | custom-call | tf_op jit(solution)/shard_map/assemble/pallas_call | solution.py:484
  (4 shorter events, 0.1 us)
Async XLA Ops:
  3.0 16.9 %collective-permute-start.1 = (bf16[4,24,64,128]{3,2,1,0:T(8,128)(2,1)S(1)}, bf16[4,24,64,128]{3,2,1,0:T(8,128)(2,1)S(1)}, u32[]{:S(2)}, u32[]{:S(2)}) collective-permute-start(bf16[4,24,64,128]{3,2,1,0:T(8,128)(2,1)S(1)} %bitcast.26), channel_id=1, source_target_pairs={{3,2},{0,1},{6,3},{1,4},{7,6},{4,5},{10,7},{5,8},{11,10},{8,9},{14... | collective-permute-start | bytes 4718600 | tf_op jit(solution)/shard_map/ppermute | solution.py:422
  7.3 8.4 %copy-start = (bf16[62,16,128]{2,1,0:T(8,128)(2,1)S(1)}, bf16[62,16,128]{2,1,0:T(8,128)(2,1)}, u32[]{:S(2)}) copy-start(bf16[62,16,128]{2,1,0:T(8,128)(2,1)} %pack.1.refs_0_) | copy-start | bytes 761860
  7.3 8.4 %copy-start.1 = (s32[2,8]{1,0:T(2,128)S(1)}, s32[2,8]{1,0:T(2,128)}, u32[]{:S(2)}) copy-start(s32[2,8]{1,0:T(2,128)} %foot_ref.5) | copy-start | bytes 196
  7.3 8.4 %collective-permute-start = (bf16[62,16,128]{2,1,0:T(8,128)(2,1)}, bf16[62,16,128]{2,1,0:T(8,128)(2,1)S(1)}, u32[]{:S(2)}, u32[]{:S(2)}) collective-permute-start(bf16[62,16,128]{2,1,0:T(8,128)(2,1)} %pack.1.refs_0_), channel_id=1, source_target_pairs={{0,2},{2,0},{1,3},{3,1},{4,6},{6,4},{5,7},{7,5},{8,10},{10,8},{9,1... | collective-permute-start | bytes 761864 | tf_op jit(solution)/shard_map/ppermute | solution.py:412
  15.7 4.1 %copy-start.2 = (s32[1,4,768]{2,1,0:T(4,128)S(1)}, s32[1,4,768]{2,1,0:T(4,128)}, u32[]{:S(2)}) copy-start(s32[1,4,768]{2,1,0:T(4,128)} %param.13) | copy-start | bytes 36868
  15.7 4.2 %copy-start.3 = (f32[64]{0:T(128)S(1)}, f32[64]{0:T(128)}, u32[]{:S(2)}) copy-start(f32[64]{0:T(128)} %param.11) | copy-start | bytes 772
  30.8 22.3 %collective-permute-start.2 = (f32[2,19,16,128]{3,2,1,0:T(8,128)S(1)}, f32[2,19,16,128]{3,2,1,0:T(8,128)S(1)}, u32[]{:S(2)}, u32[]{:S(2)}) collective-permute-start(f32[2,19,16,128]{3,2,1,0:T(8,128)S(1)} %get-tuple-element.23), channel_id=1, source_target_pairs={{0,1},{1,0},{2,3},{3,2},{4,5},{5,4},{6,7},{7,6},{8,9},{9,8},{10,11... | collective-permute-start | bytes 933896 | tf_op jit(solution)/shard_map/ppermute | solution.py:473
  53.1 8.6 %collective-permute-start.3 = (f32[19,16,128]{2,1,0:T(8,128)S(1)}, f32[19,16,128]{2,1,0:T(8,128)S(1)}, u32[]{:S(2)}, u32[]{:S(2)}) collective-permute-start(f32[19,16,128]{2,1,0:T(8,128)S(1)} %fusion), channel_id=1, source_target_pairs={{0,2},{2,0},{1,3},{3,1},{4,6},{6,4},{5,7},{7,5},{8,10},{10,8},{9,1... | collective-permute-start | bytes 466952 | tf_op jit(solution)/shard_map/ppermute | solution.py:477
  61.8 5.8 %collective-permute-start.4 = (f32[19,16,128]{2,1,0:T(8,128)S(1)}, f32[19,16,128]{2,1,0:T(8,128)S(1)}, u32[]{:S(2)}, u32[]{:S(2)}) collective-permute-start(f32[19,16,128]{2,1,0:T(8,128)S(1)} %fusion.2), channel_id=1, source_target_pairs={{0,4},{4,0},{8,12},{12,8},{1,5},{5,1},{9,13},{13,9},{2,6},{6,2},{1... | collective-permute-start | bytes 466952 | tf_op jit(solution)/shard_map/ppermute | solution.py:480
  67.6 9.1 %collective-permute-start.5 = (f32[19,16,128]{2,1,0:T(8,128)S(1)}, f32[19,16,128]{2,1,0:T(8,128)S(1)}, u32[]{:S(2)}, u32[]{:S(2)}) collective-permute-start(f32[19,16,128]{2,1,0:T(8,128)S(1)} %add.31), channel_id=1, source_target_pairs={{0,8},{4,12},{8,0},{12,4},{1,9},{5,13},{9,1},{13,5},{2,10},{6,14},... | collective-permute-start | bytes 466952 | tf_op jit(solution)/shard_map/ppermute | solution.py:480
  76.8 1.5 %copy-start.4 = (f32[19,16,128]{2,1,0:T(8,128)}, f32[19,16,128]{2,1,0:T(8,128)S(1)}, u32[]{:S(2)}) copy-start(f32[19,16,128]{2,1,0:T(8,128)S(1)} %add.32.mine_ref) | copy-start | bytes 466948
  76.8 1.4 %collective-permute-start.6 = (f32[19,16,128]{2,1,0:T(8,128)S(1)}, f32[19,16,128]{2,1,0:T(8,128)S(1)}, u32[]{:S(2)}, u32[]{:S(2)}) collective-permute-start(f32[19,16,128]{2,1,0:T(8,128)S(1)} %add.32.mine_ref), channel_id=1, source_target_pairs={{0,1},{1,0},{2,3},{3,2},{4,5},{5,4},{6,7},{7,6},{8,9},{9,8},{10,11... | collective-permute-start | bytes 466952 | tf_op jit(solution)/shard_map/ppermute | solution.py:482
  78.2 0.7 copy-start.5

commit v3 on v2

--- a/solution.py
+++ b/solution.py
@@ -164,6 +164,7 @@
     grad,
     grad_down,
     small,
+    whole,
 ):
     reps, chans = lax.axis_size("rep"), lax.axis_size("chan")
     columns = lax.axis_size("bricks") * reps
@@ -328,18 +329,7 @@
     share = 64 // chans // reps
 
     def emit(slab, value):
-        for c in range(chans):
-            place = lax.rem(c - chan + chans, chans)
-            for r in range(reps):
-                rows = value[(c * reps + r) * share : (c * reps + r + 1) * share]
-
-                @pl.when(rep == r)
-                def _():
-                    keep_ref[place, slab] = rows
-
-                @pl.when(rep != r)
-                def _():
-                    send_ref[place, slab] = rows
+        whole[slab] = value
 
     firsts = []
     for a in range(3):
@@ -364,6 +354,11 @@
     total = jnp.sum(sums[1:2], axis=1, keepdims=True) * (1.0 / 64)
     row = merge_half(head, jnp.broadcast_to(total, (1, 128)))
     emit(18, jnp.broadcast_to(row, (64, 128)))
+    for c in range(chans):
+        place = lax.rem(c - chan + chans, chans)
+        for ref, r in ((keep_ref, rep), (send_ref, 1 - rep)):
+            rows = pl.ds(pl.multiple_of((c * reps + r) * share, share), share)
+            ref[place] = whole[:, rows, :]
 
 
 def final_kernel(foot_ref, mine_ref, peer_ref, second_ref, down_ref, head_ref, loss_ref):
@@ -388,6 +383,28 @@
         live += foot_ref[1, c]
     scale = jnp.full((1, 1), COARSE * live, jnp.int32).astype(F32)
     loss_ref[...] = line[:, 64:65] / scale
+
+
+def sums_slab(shape):
+    return lax.broadcasted_iota(jnp.int32, shape, 0) == 18
+
+
+def to_wire(value):
+    high = lax.reduce_precision(value, 8, 7)
+    rest = lax.reduce_precision(value - high, 8, 7)
+    lower = lax.broadcasted_iota(jnp.int32, value.shape, 1) >= value.shape[1] // 2
+    return jnp.where(sums_slab(value.shape) & lower, rest, high)
+
+
+def from_wire(value):
+    half = value.shape[1] // 2
+    other = jnp.concatenate([value[:, half:], value[:, :half]], axis=1)
+    return value + jnp.where(sums_slab(value.shape), other, 0.0)
+
+
+def send_sum(value, axis, pairs):
+    wire = to_wire(value)
+    return from_wire(wire), from_wire(lax.ppermute(wire.astype(BF16), axis, pairs).astype(F32))
 
 
 def shards(features, w_first, w_second, w_down, w_head, footprint, labels):
@@ -463,6 +480,7 @@
             pltpu.VMEM((3, 384, 256), F32),
             pltpu.VMEM((256, 512), F32),
             pltpu.VMEM((8, 128), F32),
+            pltpu.VMEM((19, 64, 128), F32),
         ],
         compiler_params=pltpu.CompilerParams(vmem_limit_bytes=40 << 20),
         cost_estimate=pl.CostEstimate(flops=4 * 6 * 6 * 512 * 1024 * 512, bytes_accessed=16 << 20, transcendentals=0),
@@ -474,10 +492,10 @@
     mine = keep[0] + got[0]
     for step in range(1, chans):
         ring = [(i, (i + step) % chans) for i in range(chans)]
-        mine = mine + lax.ppermute(keep[step] + got[step], "chan", ring)
+        mine = mine + send_sum(keep[step] + got[step], "chan", ring)[1]
     step = 1
     while step < bricks:
-        mine = mine + lax.ppermute(mine, "bricks", [(i, i ^ step) for i in range(bricks)])
+        mine = sum(send_sum(mine, "bricks", [(i, i ^ step) for i in range(bricks)]))
         step *= 2
     peer = lax.ppermute(mine, "rep", swap)
     share = 64 // chans

time: 79.8 us -> 72.1 us (0.904); the launches traced: 80.8 us -> 71.8 us
  waiting for transfers between devices: 22.3 us -> 13 us
  starting transfers between devices: 31.9 us -> 23 us
  Pallas kernels: 18.9 us -> 27.5 us
    ppermute x1, starting transfers between devices: 21.1 us -> 0.07 us  [shards(): got = lax.ppermute(send, 'rep', swap)]
    ppermute x3, starting transfers between devices: 6.56 us -> 18.7 us  [send_sum(): lax.ppermute(wire.astype(BF16), axis, pairs).astype(F32)]
    ppermute x3, waiting for transfers between devices: 17 us -> 7.38 us  [send_sum(): lax.ppermute(wire.astype(BF16), axis, pairs).astype(F32)]
    pallas_call x1, Pallas kernels: 10.9 us -> 17.3 us  [shards(): pl.pallas_call(main_kernel, out_shape=(parts, parts), in_specs=[smem] + [...]
    pallas_call x1, Pallas kernels: 4.12 us -> 6.37 us  [shards(): pl.pallas_call(local_kernel, out_shape=(jax.ShapeDtypeStruct((4, slabs, R...]
  transfers between devices with their start and end apart: 7 -> 7, of which waited for: 6 -> 6; matrix products, arithmetic and copies ran while one was open for 5% -> 5% of each run, Pallas kernels for 7% -> 11%
where the time goes in v3:
time: 72.1 us; the launch traced here: 71.8 us
  Pallas kernels  27.5 us (38%)
  starting transfers between devices  23 us (32%)
  waiting for transfers between devices  13 us (18%)
  local copies, waits for them, and re-layouts  6.96 us (10%)
  between operations  0.8 us (1%)
    ppermute x3, starting transfers between devices, send_sum(): lax.ppermute(wire.astype(BF16), axis, pairs).astype(F32)  18.7 us
    pallas_call x1, Pallas kernels, shards(): pl.pallas_call(main_kernel, out_shape=(parts, parts), in_specs=[smem] + [...  17.3 us
    ppermute x3, waiting for transfers between devices, send_sum(): lax.ppermute(wire.astype(BF16), axis, pairs).astype(F32)  7.38 us
    pallas_call x1, Pallas kernels, shards(): pl.pallas_call(local_kernel, out_shape=(jax.ShapeDtypeStruct((4, slabs, R...  6.37 us
    unnamed x13, local copies, waits for them, and re-layouts  4.6 us
    ppermute x1, waiting for transfers between devices, shards(): pieces.append(lax.ppermute(packed, 'chan', ring))  2.72 us
    ppermute x1, starting transfers between devices, shards(): halo = lax.ppermute(outward, ('bricks', 'chan', 'rep'), pairs)  2.46 us
    dynamic_slice x2, local copies, waits for them, and re-layouts, shards(): lax.dynamic_slice_in_dim(features, (1 - side) * 4, 4, 1)  2.3 us
  transfers between devices with their start and end apart: 7, of which 6 were waited for; matrix products, arithmetic and copies ran while one was open for 5% of the time, Pallas kernels for 11%

profile of v3, /device:TPU:0, one launch (start us, length us, event | category | flops | bytes accessed | tf_op | source)
XLA Modules:
  0.0 71.8 jit_solution(17157370178199587213)
XLA Ops:
  0.6 1.7 %constant_dynamic-slice_fusion = bf16[1,64,4,24,128]{4,3,2,1,0:T(8,128)(2,1)S(1)} fusion(bf16[1,64,8,24,128]{4,3,2,1,0:T(8,128)(2,1)} %param.7, s32[]{:T(128)S(6)} %select_n.35), kind=kLoop, calls=%fused_computation.31 | loop fusion | bytes 3145732 | tf_op jit(solution)/shard_map/dynamic_slice | solution.py:438
  2.3 0.6 copy.16
  3.0 2.5 %collective-permute-start.1 = (bf16[4,24,64,128]{3,2,1,0:T(8,128)(2,1)S(1)}, bf16[4,24,64,128]{3,2,1,0:T(8,128)(2,1)S(1)}, u32[]{:S(2)}, u32[]{:S(2)}) collective-permute-start(bf16[4,24,64,128]{3,2,1,0:T(8,128)(2,1)S(1)} %bitcast.31), channel_id=1, source_target_pairs={{3,2},{0,1},{6,3},{1,4},{7,6},{4,5},{10,7},{5,8},{11,10},{8,9},{14... | collective-permute-start | bytes 4718600 | tf_op jit(solution)/shard_map/ppermute | solution.py:439
  5.4 1.9 %pack.1.refs_0_ = bf16[62,16,128]{2,1,0:T(8,128)(2,1)} custom-call(bf16[27,32,64]{2,1,0:T(8,128)(2,1)} %bitcast.32, bf16[27,32,64]{2,1,0:T(8,128)(2,1)} %bitcast.33, bf16[8,32,64]{2,1,0:T(8,128)(2,1)} %wd_ref.1), custom_call_target="tpu_custom_call" | custom-call | tf_op jit(solution)/shard_map/pack/pallas_call | solution.py:419
  7.3 0.0 copy-start
  7.3 0.0 copy-start.1
  7.3 1.8 %collective-permute-start = (bf16[62,16,128]{2,1,0:T(8,128)(2,1)}, bf16[62,16,128]{2,1,0:T(8,128)(2,1)S(1)}, u32[]{:S(2)}, u32[]{:S(2)}) collective-permute-start(bf16[62,16,128]{2,1,0:T(8,128)(2,1)} %pack.1.refs_0_), channel_id=1, source_target_pairs={{0,2},{2,0},{1,3},{3,1},{4,6},{6,4},{5,7},{7,5},{8,10},{10,8},{9,1... | collective-permute-start | bytes 761864 | tf_op jit(solution)/shard_map/ppermute | solution.py:429
  9.1 3.9 %copy.15 = bf16[1,64,8,24,128]{4,1,3,2,0:T(8,128)(2,1)S(1)} copy(bf16[1,64,8,24,128]{4,3,2,1,0:T(8,128)(2,1)} %param.7) | data formatting | bytes 6291456 | tf_op args[0]
  13.0 2.7 %collective-permute-done.refs_1_ = bf16[62,16,128]{2,1,0:T(8,128)(2,1)S(1)} collective-permute-done((bf16[62,16,128]{2,1,0:T(8,128)(2,1)}, bf16[62,16,128]{2,1,0:T(8,128)(2,1)S(1)}, u32[]{:S(2)}, u32[]{:S(2)}) %collective-permute-start) | collective-permute-done | bytes 253984 | tf_op jit(solution)/shard_map/ppermute | solution.py:429
  15.7 0.0 copy-done
  15.7 0.0 copy-done.1
  15.7 0.0 copy-start.2
  15.7 0.0 copy-start.3
  15.7 6.4 %first_local.1 = (bf16[4,6,256,128]{3,2,1,0:T(8,128)(2,1)S(1)}, bf16[4,6,256,128]{3,2,1,0:T(8,128)(2,1)S(1)}, bf16[3,1024,256]{2,1,0:T(8,128)(2,1)S(1)}, bf16[3,...) custom-call(s32[2,8]{1,0:T(2,128)S(1)} %copy-done.1, ...), custom_call_target="tpu_custom_call" | custom-call | flops 9663676416 | bytes 8388608 | tf_op jit(solution)/shard_map/first_local/pallas_call | solution.py:441
  22.1 0.0 collective-permute-done.1.halo_ref
  22.1 0.0 copy-done.2
  22.1 0.0 copy-done.3
  22.1 17.3 %head_and_grads.1 = (f32[2,19,16,128]{3,2,1,0:T(8,128)S(1)}, f32[2,19,16,128]{3,2,1,0:T(8,128)S(1)}) custom-call(s32[2,8]{1,0:T(2,128)S(1)} %copy-done.1, bf16[4,6,256,128]{3,2,1,0:T(8,128)(2,1)S(1)} %get-tuple-element.16.edge_ref, bf16[4,24,64,128]{3,2,1,0:T(8,128)(2,1)S(1)} %collective-permute-done.1.halo_ref, ...), custom_call_target="tpu_custom_call" | custom-call | flops 38654705664 | bytes 16777216 | tf_op jit(solution)/shard_map/head_and_grads/pallas_call | solution.py:465
  39.5 0.1 collective-permute-start.2
  39.6 1.6 %collective-permute-done.2 = f32[2,19,16,128]{3,2,1,0:T(8,128)S(1)} collective-permute-done((f32[2,19,16,128]{3,2,1,0:T(8,128)S(1)}, f32[2,19,16,128]{3,2,1,0:T(8,128)S(1)}, u32[]{:S(2)}, u32[]{:S(2)}) %collective-permute-start.2) | collective-permute-done | bytes 311328 | tf_op jit(solution)/shard_map/ppermute | solution.py:491
  41.1 0.1 fusion.3
  41.2 2.7 %collective-permute-start.3 = (bf16[19,16,128]{2,1,0:T(8,128)(2,1)S(1)}, bf16[19,16,128]{2,1,0:T(8,128)(2,1)S(1)}, u32[]{:S(2)}, u32[]{:S(2)}) collective-permute-start(bf16[19,16,128]{2,1,0:T(8,128)(2,1)S(1)} %fusion.3), channel_id=1, source_target_pairs={{0,2},{2,0},{1,3},{3,1},{4,6},{6,4},{5,7},{7,5},{8,10},{10,8},{9,1... | collective-permute-start | bytes 233480 | tf_op jit(solution)/shard_map/ppermute | solution.py:407
  43.9 2.7 %collective-permute-done.3 = bf16[19,16,128]{2,1,0:T(8,128)(2,1)S(1)} collective-permute-done((bf16[19,16,128]{2,1,0:T(8,128)(2,1)S(1)}, bf16[19,16,128]{2,1,0:T(8,128)(2,1)S(1)}, u32[]{:S(2)}, u32[]{:S(2)}) %collective-permute-start.3) | collective-permute-done | bytes 77856 | tf_op jit(solution)/shard_map/ppermute | solution.py:407
  46.6 0.1 fusion.15
  46.7 4.6 %collective-permute-start.4 = (bf16[19,16,128]{2,1,0:T(8,128)(2,1)S(1)}, bf16[19,16,128]{2,1,0:T(8,128)(2,1)S(1)}, u32[]{:S(2)}, u32[]{:S(2)}) collective-permute-start(bf16[19,16,128]{2,1,0:T(8,128)(2,1)S(1)} %get-tuple-element.30), channel_id=1, source_target_pairs={{0,4},{4,0},{8,12},{12,8},{1,5},{5,1},{9,13},{13,9},{2,6},{6,2},{1... | collective-permute-start | bytes 233480 | tf_op jit(solution)/shard_map/ppermute | solution.py:407
  51.3 2.4 %collective-permute-done.4 = bf16[19,16,128]{2,1,0:T(8,128)(2,1)S(1)} collective-permute-done((bf16[19,16,128]{2,1,0:T(8,128)(2,1)S(1)}, bf16[19,16,128]{2,1,0:T(8,128)(2,1)S(1)}, u32[]{:S(2)}, u32[]{:S(2)}) %collective-permute-start.4) | collective-permute-done | bytes 77856 | tf_op jit(solution)/shard_map/ppermute | solution.py:407
  53.7 0.1 fusion.14
  53.9 11.4 %collective-permute-start.5 = (bf16[19,16,128]{2,1,0:T(8,128)(2,1)S(1)}, bf16[19,16,128]{2,1,0:T(8,128)(2,1)S(1)}, u32[]{:S(2)}, u32[]{:S(2)}) collective-permute-start(bf16[19,16,128]{2,1,0:T(8,128)(2,1)S(1)} %get-tuple-element.28), channel_id=1, source_target_pairs={{0,8},{4,12},{8,0},{12,4},{1,9},{5,13},{9,1},{13,5},{2,10},{6,14},... | collective-permute-start | bytes 233480 | tf_op jit(solution)/shard_map/ppermute | solution.py:407
  65.3 2.4 %collective-permute-done.5 = bf16[19,16,128]{2,1,0:T(8,128)(2,1)S(1)} collective-permute-done((bf16[19,16,128]{2,1,0:T(8,128)(2,1)S(1)}, bf16[19,16,128]{2,1,0:T(8,128)(2,1)S(1)}, u32[]{:S(2)}, u32[]{:S(2)}) %collective-permute-start.5) | collective-permute-done | bytes 77856 | tf_op jit(solution)/shard_map/ppermute | solution.py:407
  67.6 0.1 fusion.12.mine_ref
  67.8 0.0 copy-start.4
  67.8 0.1 collective-permute-start.6
  67.8 1.4 %collective-permute-done.6.peer_ref = f32[19,16,128]{2,1,0:T(8,128)S(1)} collective-permute-done((f32[19,16,128]{2,1,0:T(8,128)S(1)}, f32[19,16,128]{2,1,0:T(8,128)S(1)}, u32[]{:S(2)}, u32[]{:S(2)}) %collective-permute-start.6) | collective-permute-done | bytes 155680 | tf_op jit(solution)/shard_map/ppermute | solution.py:500
  69.2 0.0 copy-done.4
  69.2 0.0 copy-start.5
  69.2 0.7 copy-done.5
  69.9 1.9 %assemble.1 = (f32[27,32,64]{2,1,0:T(8,128)}, f32[8,32,64]{2,1,0:T(8,128)}, f32[1,64]{1,0:T(1,128)}, f32[1,1]{1,0:T(1,128)}) custom-call(s32[2,8]{1,0:T(2,128)} %foot_ref.5, f32[19,16,128]{2,1,0:T(8,128)} %copy-done.4, f32[19,16,128]{2,1,0:T(8,128)} %copy-done.5), custom_call_target="tpu_custom_call" | custom-call | tf_op jit(solution)/shard_map/assemble/pallas_call | solution.py:502
  (7 shorter events, 0.1 us)
Async XLA Ops:
  3.0 19.2 %collective-permute-start.1 = (bf16[4,24,64,128]{3,2,1,0:T(8,128)(2,1)S(1)}, bf16[4,24,64,128]{3,2,1,0:T(8,128)(2,1)S(1)}, u32[]{:S(2)}, u32[]{:S(2)}) collective-permute-start(bf16[4,24,64,128]{3,2,1,0:T(8,128)(2,1)S(1)} %bitcast.31), channel_id=1, source_target_pairs={{3,2},{0,1},{6,3},{1,4},{7,6},{4,5},{10,7},{5,8},{11,10},{8,9},{14... | collective-permute-start | bytes 4718600 | tf_op jit(solution)/shard_map/ppermute | solution.py:439
  7.3 8.4 %copy-start = (bf16[62,16,128]{2,1,0:T(8,128)(2,1)S(1)}, bf16[62,16,128]{2,1,0:T(8,128)(2,1)}, u32[]{:S(2)}) copy-start(bf16[62,16,128]{2,1,0:T(8,128)(2,1)} %pack.1.refs_0_) | copy-start | bytes 761860
  7.3 8.4 %copy-start.1 = (s32[2,8]{1,0:T(2,128)S(1)}, s32[2,8]{1,0:T(2,128)}, u32[]{:S(2)}) copy-start(s32[2,8]{1,0:T(2,128)} %foot_ref.5) | copy-start | bytes 196
  7.3 8.4 %collective-permute-start = (bf16[62,16,128]{2,1,0:T(8,128)(2,1)}, bf16[62,16,128]{2,1,0:T(8,128)(2,1)S(1)}, u32[]{:S(2)}, u32[]{:S(2)}) collective-permute-start(bf16[62,16,128]{2,1,0:T(8,128)(2,1)} %pack.1.refs_0_), channel_id=1, source_target_pairs={{0,2},{2,0},{1,3},{3,1},{4,6},{6,4},{5,7},{7,5},{8,10},{10,8},{9,1... | collective-permute-start | bytes 761864 | tf_op jit(solution)/shard_map/ppermute | solution.py:429
  15.7 6.4 %copy-start.2 = (s32[1,4,768]{2,1,0:T(4,128)S(1)}, s32[1,4,768]{2,1,0:T(4,128)}, u32[]{:S(2)}) copy-start(s32[1,4,768]{2,1,0:T(4,128)} %param.13) | copy-start | bytes 36868
  15.7 6.4 %copy-start.3 = (f32[64]{0:T(128)S(1)}, f32[64]{0:T(128)}, u32[]{:S(2)}) copy-start(f32[64]{0:T(128)} %param.11) | copy-start | bytes 772
  39.5 1.7 %collective-permute-start.2 = (f32[2,19,16,128]{3,2,1,0:T(8,128)S(1)}, f32[2,19,16,128]{3,2,1,0:T(8,128)S(1)}, u32[]{:S(2)}, u32[]{:S(2)}) collective-permute-start(f32[2,19,16,128]{3,2,1,0:T(8,128)S(1)} %get-tuple-element.23), channel_id=1, source_target_pairs={{0,1},{1,0},{2,3},{3,2},{4,5},{5,4},{6,7},{7,6},{8,9},{9,8},{10,11... | collective-permute-start | bytes 933896 | tf_op jit(solution)/shard_map/ppermute | solution.py:491
  41.2 5.3 %collective-permute-start.3 = (bf16[19,16,128]{2,1,0:T(8,128)(2,1)S(1)}, bf16[19,16,128]{2,1,0:T(8,128)(2,1)S(1)}, u32[]{:S(2)}, u32[]{:S(2)}) collective-permute-start(bf16[19,16,128]{2,1,0:T(8,128)(2,1)S(1)} %fusion.3), channel_id=1, source_target_pairs={{0,2},{2,0},{1,3},{3,1},{4,6},{6,4},{5,7},{7,5},{8,10},{10,8},{9,1... | collective-permute-start | bytes 233480 | tf_op jit(solution)/shard_map/ppermute | solution.py:407
  46.7 7.0 %collective-permute-start.4 = (bf16[19,16,128]{2,1,0:T(8,128)(2,1)S(1)}, bf16[19,16,128]{2,1,0:T(8,128)(2,1)S(1)}, u32[]{:S(2)}, u32[]{:S(2)}) collective-permute-start(bf16[19,16,128]{2,1,0:T(8,128)(2,1)S(1)} %get-tuple-element.30), channel_id=1, source_target_pairs={{0,4},{4,0},{8,12},{12,8},{1,5},{5,1},{9,13},{13,9},{2,6},{6,2},{1... | collective-permute-start | bytes 233480 | tf_op jit(solution)/shard_map/ppermute | solution.py:407
  53.9 13.8 %collective-permute-start.5 = (bf16[19,16,128]{2,1,0:T(8,128)(2,1)S(1)}, bf16[19,16,128]{2,1,0:T(8,128)(2,1)S(1)}, u32[]{:S(2)}, u32[]{:S(2)}) collective-permute-start(bf16[19,16,128]{2,1,0:T(8,128)(2,1)S(1)} %get-tuple-element.28), channel_id=1, source_target_pairs={{0,8},{4,12},{8,0},{12,4},{1,9},{5,13},{9,1},{13,5},{2,10},{6,14},... | collective-permute-start | bytes 233480 | tf_op jit(solution)/shard_map/ppermute | solution.py:407
  67.8 1.5 %copy-start.4 = (f32[19,16,128]{2,1,0:T(8,128)}, f32[19,16,128]{2,1,0:T(8,128)S(1)}, u32[]{:S(2)}) copy-start(f32[19,16,128]{2,1,0:T(8,128)S(1)} %fusion.12.mine_ref) | copy-start | bytes 466948
  67.8 1.4 %collective-permute-start.6 = (f32[19,16,128]{2,1,0:T(8,128)S(1)}, f32[19,16,128]{2,1,0:T(8,128)S(1)}, u32[]{:S(2)}, u32[]{:S(2)}) collective-permute-start(f32[19,16,128]{2,1,0:T(8,128)S(1)} %fusion.12.mine_ref), channel_id=1, source_target_pairs={{0,1},{1,0},{2,3},{3,2},{4,5},{5,4},{6,7},{7,6},{8,9},{9,8},{10,11... | collective-permute-start | bytes 466952 | tf_op jit(solution)/shard_map/ppermute | solution.py:500
  69.2 0.7 copy-start.5
